TPU v7x, 256 devices: a whole 4x4x8 slice. The times are simulated.
256 devices in a mesh: imp: 32 (over z, y_hi, core), cre: 8 (over x, y_lo).
Axes of the slice: x: 4, y: 4 (y_hi: 2, y_lo: 2; y = y_hi * 2 + y_lo), z: 8, core: 2. Of those that a mesh axis runs over, the one named last changes fastest.
Arguments:
- impressions: bfloat16 [32768, 256], P('imp'), may hold values from -24 to 24
- panels: bfloat16 [8, 2048, 256], P('cre', 'imp'), may hold values from -2 to 2
- block_lists: int32 [256, 16], P('imp'), may hold values from 0 to 127, as said below
- block_counts: int32 [256], P('imp'), may hold values from 1 to 16, as said below
- imp_weight: float32 [32768], P('imp'), may hold values from 0.2 to 5
- spend_goals: float32 [8, 2048], P('cre', 'imp'), may hold values from 0.2 to 5
- prices: float32 [8, 2048], P('cre', 'imp'), may hold values from -1 to 1
Outputs:
- final_prices: float32 [8, 2048], P('cre', 'imp')
- final_spend: float32 [8, 2048], P('cre', 'imp')
- log_norm: float32 [32768], P('imp')
Inputs may be any that keep to these rules, and one draw needn't show every extreme that they name: `block_lists`: each row lists 16 different block ids; only the first block_counts entries of a row are eligible for the 128 impressions of that tile, the others must be ignored. `block_counts`: some tile has 16 eligible blocks.
All inputs are finite; a program needn't handle non-finite values.
Results may differ from a plain program's by a relative error of at most 0.0003.
Values may be sent and summed in bfloat16 or wider, within the bound.
A program may use at most 64 MiB of HBM per device.

v0:
```python
import jax
import jax.numpy as jnp
from jax import lax
from jax.sharding import PartitionSpec as P

CRE_LOC = 2048
TILE = 128
BLOCK = 128
ITERS = 2


NEG_FILL = -1e30
TAU_INV = 4.0
STEP_RATE = 0.5


def block_table(block_lists, block_counts, local_blocks, cre_index):
    block_ids = cre_index * local_blocks + lax.iota(jnp.int32, local_blocks)
    in_list = lax.iota(jnp.int32, block_lists.shape[1])[None, :] < block_counts[:, None]
    matches = (block_lists[:, :, None] == block_ids[None, None, :]) & in_list[:, :, None]
    allowed = jnp.any(matches, axis=1)
    allowed = jnp.repeat(allowed, TILE, axis=0)
    return jnp.repeat(allowed, BLOCK, axis=1)


def scored(impressions, panel_rows, price_rows, col_mask):
    affinity = lax.dot_general(
        impressions, panel_rows, (((1,), (1,)), ((), ())), preferred_element_type=jnp.float32
    )
    logit_vals = TAU_INV * affinity + price_rows[None, :]
    return jnp.where(col_mask, logit_vals, NEG_FILL)


def sweep(panel_rows, group_prices, mask_full, running, update):
    col_count = panel_rows.shape[0]
    sub_width = 512

    def inner(current, step_index):
        shift_cols = step_index * sub_width
        part_panel = lax.dynamic_slice_in_dim(panel_rows, shift_cols, sub_width, 0)
        part_price = lax.dynamic_slice_in_dim(group_prices, shift_cols, sub_width, 0)
        part_mask = lax.dynamic_slice_in_dim(mask_full, shift_cols, sub_width, 1)
        return (update(current, part_panel, part_price, part_mask, shift_cols), None)

    current, _ = lax.scan(inner, running, jnp.arange(col_count // sub_width, dtype=jnp.int32))
    return current


def shards(impressions, panels, block_lists, block_counts, imp_weight, spend_goals, prices):
    local_blocks = CRE_LOC // BLOCK
    mask_full = block_table(block_lists, block_counts, local_blocks, lax.axis_index("cre"))
    imp_rows = impressions.shape[0]
    owned_rows = prices.shape[1]
    owned_start = lax.axis_index("imp") * owned_rows

    def max_step(current, panel_rows, price_rows, col_mask, first_col):
        row_top, row_total = current
        masked = scored(impressions, panel_rows, price_rows, col_mask)
        block_top = jnp.max(masked, axis=1)
        new_top = jnp.maximum(row_top, block_top)
        block_sum = jnp.sum(jnp.where(col_mask, jnp.exp(masked - block_top[:, None]), 0.0), axis=1)
        return (
            new_top,
            row_total * jnp.exp(row_top - new_top) + block_sum * jnp.exp(block_top - new_top),
        )

    spend_owned = None
    row_norm = None
    for iteration in range(ITERS):
        start_state = (
            jnp.full((imp_rows,), NEG_FILL, jnp.float32),
            jnp.zeros((imp_rows,), jnp.float32),
        )
        empty_spend = jnp.zeros((CRE_LOC,), jnp.float32)
        whole_prices = lax.all_gather(prices, "imp", axis=1, tiled=True)[0]
        row_top, row_total = sweep(
            lax.all_gather(panels, "imp", axis=1, tiled=True)[0],
            whole_prices,
            mask_full,
            start_state,
            max_step,
        )
        merged_top = lax.pmax(row_top, "cre")
        row_total = lax.psum(row_total * jnp.exp(row_top - merged_top), "cre")
        row_top = merged_top
        row_norm = row_top + jnp.log(row_total)

        def spend_step(current, panel_rows, price_rows, col_mask, first_col):
            masked = scored(impressions, panel_rows, price_rows, col_mask)
            shares = jnp.where(col_mask, jnp.exp(masked - row_norm[:, None]), 0.0)
            col_spend = jnp.sum(imp_weight[:, None] * shares, axis=0)
            return lax.dynamic_update_slice_in_dim(current, col_spend, first_col, 0)

        partial_spend = sweep(
            lax.all_gather(panels, "imp", axis=1, tiled=True)[0],
            whole_prices,
            mask_full,
            empty_spend,
            spend_step,
        )
        summed = lax.psum(partial_spend, "imp")
        spend_owned = lax.dynamic_slice_in_dim(summed, owned_start, owned_rows, 0)
        spend_owned = spend_owned.reshape(1, owned_rows)
        prices = prices + STEP_RATE * (
            jnp.log(spend_goals) - jnp.log(spend_owned + 0.25 * spend_goals)
        )
    return (prices, spend_owned, row_norm)


def solution(mesh):
    placed = (
        P("imp", None),
        P("cre", "imp", None),
        P("imp", None),
        P("imp"),
        P("imp"),
        P("cre", "imp"),
        P("cre", "imp"),
    )
    return jax.shard_map(
        shards,
        mesh=mesh,
        in_specs=placed,
        out_specs=(P("cre", "imp"), P("cre", "imp"), P("imp")),
        check_vma=False,
    )
```

profile of v0, /device:TPU:1, one launch (start us, length us, event | category | flops | bytes accessed | tf_op | source)
XLA Modules:
  0.0 427.9 jit_solution(15510092804575440473)
XLA Ops:
  7.2 0.7 all-gather.2.cloned.1.call-update
  8.0 0.7 iota_compare_fusion
  8.7 0.8 and_reduce_fusion
  9.7 1.3 dynamic-slice
  11.6 0.8 bitcast_dynamic-update-slice_fusion.1
  12.4 70.3 %all-reduce = f32[2048]{0:T(1024)S(1)} all-reduce(f32[2048]{0:T(1024)S(1)} %bitcast_dynamic-update-slice_fusion.1), channel_id=1, replica_groups=mesh['imp'=32,'cre'=8] {'imp'}, use_global_device_ids=true, to_apply=%add | all-reduce | flops 2048 | bytes 16384 | tf_op jit(solution)/shard_map/squeeze | solution.py:75
  82.8 9.8 %all-gather.2.cloned.1.call-done = bf16[1,2048,256]{2,1,0:T(8,128)(2,1)} async-done(((bf16[1,64,256]{2,1,0:T(8,128)(2,1)}), bf16[1,2048,256]{2,1,0:T(8,128)(2,1)}) %all-gather.2.cloned.1.call-update) | async-done | bytes 1048592 | tf_op jit(solution)/shard_map/all_gather | solution.py:95
  93.1 0.7 copy-done.3
  93.7 15.7 %while.48 = (s32[]{:T(128)}, f32[1024]{0:T(1024)S(1)}, f32[1024]{0:T(1024)S(1)}, s32[4]{0:T(128)S(1)}, pred[1024,2048]{0,1:T(32,128)(4,1)S(1)}, /*index=5*/bf16[...) while((s32[]{:T(128)}, f32[1024]{0:T(1024)S(1)}, ...), condition=%wide.region_4.5_spmd.clone, body=%wide.region_1.4_spmd.clone.sunk | while | flops 273684480 | bytes 6075585 | solution.py:45
  93.8 0.7 dynamic_slice.118
  95.2 1.7 fusion.49
  96.9 0.8 select_reduce_fusion.4
  97.7 0.7 dynamic_slice.118
  99.1 1.7 fusion.49
  100.8 0.8 select_reduce_fusion.4
  101.6 0.7 dynamic_slice.118
  103.0 1.7 fusion.49
  104.7 0.8 select_reduce_fusion.4
  105.5 0.7 dynamic_slice.118
  107.0 1.7 fusion.49
  108.6 0.8 select_reduce_fusion.4
  109.4 14.9 %pmax.14 = f32[1024]{0:T(1024)S(1)} all-reduce(f32[1024]{0:T(1024)S(1)} %get-tuple-element.183), channel_id=1, replica_groups=mesh['imp'=32,'cre'=8] {'cre'}, use_global_device_ids=true, to_apply=%region_5.6 | all-reduce | flops 1024 | bytes 8192 | tf_op jit(solution)/shard_map/pmax | solution.py:83
  124.4 12.5 %psum.28 = f32[1024]{0:T(1024)S(1)} all-reduce(f32[1024]{0:T(1024)S(1)} %exponential_multiply_fusion.1), channel_id=1, replica_groups=mesh['imp'=32,'cre'=8] {'cre'}, use_global_device_ids=true, to_apply=%region_6.7 | all-reduce | flops 1024 | bytes 8192 | tf_op jit(solution)/shard_map/psum | solution.py:84
  136.9 14.6 %while.46 = (s32[]{:T(128)}, f32[2048]{0:T(1024)S(1)}, f32[1024]{0:T(1024)S(1)}, s32[4]{0:T(128)S(1)}, pred[1024,2048]{0,1:T(32,128)(4,1)S(1)}, /*index=5*/bf16[...) while((s32[]{:T(128)}, f32[2048]{0:T(1024)S(1)}, ...), condition=%wide.region_9.10_spmd, body=%wide.region_7.9_spmd.sunk | while | flops 272104960 | bytes 1332415 | solution.py:45
  138.2 2.1 fusion.44
  141.9 2.1 fusion.44
  145.6 2.1 fusion.44
  149.2 2.1 fusion.44
  151.5 72.9 %psum.29 = f32[2048]{0:T(1024)S(1)} all-reduce(f32[2048]{0:T(1024)S(1)} %get-tuple-element.185), channel_id=1, replica_groups=mesh['imp'=32,'cre'=8] {'imp'}, use_global_device_ids=true, to_apply=%region_10.11 | all-reduce | flops 2048 | bytes 16384 | tf_op jit(solution)/shard_map/psum | solution.py:101
  224.6 66.0 %all-reduce.1 = f32[2048]{0:T(1024)S(1)} all-reduce(f32[2048]{0:T(1024)S(1)} %get-tuple-element.317), channel_id=1, replica_groups=mesh['imp'=32,'cre'=8] {'imp'}, use_global_device_ids=true, to_apply=%add.1 | all-reduce | flops 2048 | bytes 16384 | tf_op jit(solution)/shard_map/squeeze | solution.py:75
  290.7 15.2 %while.49 = (s32[]{:T(128)}, f32[1024]{0:T(1024)S(1)}, f32[1024]{0:T(1024)S(1)}, s32[4]{0:T(128)S(1)}, pred[1024,2048]{0,1:T(32,128)(4,1)S(1)}, /*index=5*/bf16[...) while((s32[]{:T(128)}, f32[1024]{0:T(1024)S(1)}, ...), condition=%wide.region_14.15_spmd.clone, body=%wide.region_11.14_spmd.clone.sunk | while | flops 273684480 | bytes 6075585 | solution.py:45
  292.0 1.7 fusion.52
  293.7 0.8 select_reduce_fusion.5
  295.8 1.7 fusion.52
  297.5 0.8 select_reduce_fusion.5
  299.6 1.7 fusion.52
  301.3 0.8 select_reduce_fusion.5
  303.4 1.7 fusion.52
  305.1 0.8 select_reduce_fusion.5
  305.9 14.2 %pmax.15 = f32[1024]{0:T(1024)S(1)} all-reduce(f32[1024]{0:T(1024)S(1)} %get-tuple-element.186), channel_id=1, replica_groups=mesh['imp'=32,'cre'=8] {'cre'}, use_global_device_ids=true, to_apply=%region_15.16 | all-reduce | flops 1024 | bytes 8192 | tf_op jit(solution)/shard_map/pmax | solution.py:83
  320.0 12.8 %psum.30 = f32[1024]{0:T(1024)S(1)} all-reduce(f32[1024]{0:T(1024)S(1)} %exponential_multiply_fusion), channel_id=1, replica_groups=mesh['imp'=32,'cre'=8] {'cre'}, use_global_device_ids=true, to_apply=%region_16.17 | all-reduce | flops 1024 | bytes 8192 | tf_op jit(solution)/shard_map/psum | solution.py:84
  332.8 14.6 %while.47 = (s32[]{:T(128)}, f32[2048]{0:T(1024)S(1)}, f32[1024]{0:T(1024)S(1)}, s32[4]{0:T(128)S(1)}, pred[1024,2048]{0,1:T(32,128)(4,1)S(1)}, /*index=5*/bf16[...) while((s32[]{:T(128)}, f32[2048]{0:T(1024)S(1)}, ...), condition=%wide.region_19.20_spmd, body=%wide.region_17.19_spmd.sunk | while | flops 272104960 | bytes 1332415 | solution.py:45
  334.1 2.1 fusion.47
  337.8 2.1 fusion.47
  341.5 2.1 fusion.47
  345.1 2.1 fusion.47
  347.4 73.0 %psum.31 = f32[2048]{0:T(1024)S(1)} all-reduce(f32[2048]{0:T(1024)S(1)} %get-tuple-element.188), channel_id=1, replica_groups=mesh['imp'=32,'cre'=8] {'imp'}, use_global_device_ids=true, to_apply=%region_20.21 | all-reduce | flops 2048 | bytes 16384 | tf_op jit(solution)/shard_map/psum | solution.py:101
  420.5 0.6 multiply_add_fusion
  (76 shorter events, 11.5 us)
Async XLA Ops:
  7.2 85.4 %all-gather.2.cloned.1.call-start = ((), (), s32[]{:S(2)}) async-start(), calls=%async_computation | async-start | bytes 1081344 | tf_op jit(solution)/shard_map/all_gather | solution.py:95
  92.5 1.2 copy-start.3
  93.7 43.1 %copy-start.4 = (f32[1024]{0:T(1024)S(1)}, f32[1024]{0:T(1024)}, u32[]{:S(2)}) copy-start(f32[1024]{0:T(1024)} %param.19) | copy-start | bytes 12292
  136.9 87.5 %copy-start.1 = (f32[1,64]{1,0:T(1,128)S(1)}, f32[1,64]{1,0:T(1,128)}, u32[]{:S(2)}) copy-start(f32[1,64]{1,0:T(1,128)} %param.20) | copy-start | bytes 772
  136.9 87.5 %copy-start.2 = (f32[1,64]{1,0:T(1,128)S(1)}, f32[1,64]{1,0:T(1,128)}, u32[]{:S(2)}) copy-start(f32[1,64]{1,0:T(1,128)} %param.21) | copy-start | bytes 772
  347.4 73.7 %copy-start = (f32[1024]{0:T(1024)}, f32[1024]{0:T(1024)S(1)}, u32[]{:S(2)}) copy-start(f32[1024]{0:T(1024)S(1)} %get-tuple-element.705) | copy-start | bytes 12292
Sparse Core Ops, SparseCore 0:
  10.8 81.6 all-gather.1
where the time goes:
time: 429 us; the launch traced here: 428 us
  blocking collectives  337 us (79%)
  matrix products  29.8 us (7%)
  local copies, waits for them, and re-layouts  16.5 us (4%)
  between operations  14.9 us (3%)
  loops' own time  11 us (3%)
  waiting for transfers between devices  10.4 us (2%)
  other arithmetic  8.58 us (2%)
    psum x2, blocking collectives, shards(): summed = lax.psum(partial_spend, 'imp')  146 us
    squeeze x2, blocking collectives, shards(): whole_prices = lax.all_gather(prices, 'imp', axis=1, tiled=True)[0]  136 us
    dot_general x16, matrix products, scored(): lax.dot_general(impressions, panel_rows, (((1,), (1,)), ((), ())), prefer...  29.8 us
    pmax x2, blocking collectives, shards(): merged_top = lax.pmax(row_top, 'cre')  29.1 us
    psum x2, blocking collectives, shards(): row_total = lax.psum(row_total * jnp.exp(row_top - merged_top), 'cre')  25.2 us
    another operation x4, loops' own time, sweep(): lax.scan(inner, running, jnp.arange(col_count // sub_width, dtype=jnp.int...  11 us
    all_gather x1, waiting for transfers between devices, shards(): lax.all_gather(panels, 'imp', axis=1, tiled=True)[0]  9.76 us
    dynamic_slice x16, local copies, waits for them, and re-layouts, sweep(): lax.scan(inner, running, jnp.arange(col_count // sub_width, dtype=jnp.int...  9.67 us
  transfers between devices with their start and end apart: 1, of which 1 were waited for; matrix products, arithmetic and copies ran while one was open for 1% of the time, Pallas kernels for 0%

commit v1 on v0

v1 whole, which is shorter than its diff:
```python
import functools
import math

import jax
import jax.numpy as jnp
from jax import lax
from jax.experimental import pallas as pl
from jax.experimental.pallas import tpu as pltpu
from jax.sharding import PartitionSpec as P

MESH = pl.DeviceIdType.MESH
F32 = jnp.float32
TILE = 128
NEG_FILL = -1e30
TAU_INV = 4.0
STEP_RATE = 0.5
EXP2_SCALE = TAU_INV * math.log2(math.e)


def kernel(
    n_chip,
    n_cre,
    imp_hbm,
    panel_hbm,
    list_hbm,
    count_ref,
    weight_hbm,
    goal_hbm,
    price_hbm,
    new_price_ref,
    spend_ref,
    norm_ref,
    imps,
    panels,
    kmat,
    top,
    zsum,
    bias,
    rmat,
    vcol,
    wl,
    lists,
    pg_own,
    pg,
    mx_row,
    zt_row,
    lse,
    norms,
    part1,
    part2,
    got2,
    local_sem,
    panel_send,
    right_sem,
    left_sem,
    pair_sem,
    pg_send,
    pg_recv,
    core_send,
    core_recv,
    x_send,
    x_recv,
    y_send,
    y_recv,
):
    i = lax.axis_index("imp")
    g = lax.axis_index("cre")
    c = lax.rem(i, 2)
    q = i // 2
    y = lax.rem(q, 2)
    z = q // 2
    nz = n_chip // 2
    half = nz // 2
    n_x = n_cre * 2
    me_x = g * 2 + c
    rows = imp_hbm.shape[0]
    width = panel_hbm.shape[0]
    tiles = 2 * rows // TILE
    own_tiles = tiles // 2
    packed = n_chip // 2

    def chip_peer(k):
        other = lax.rem(q + k, n_chip)
        return other, {"imp": other * 2 + c, "cre": g}

    def cre_peer(k):
        other = lax.rem(me_x + k, n_x)
        return {"imp": q * 2 + lax.rem(other, 2), "cre": other // 2}

    def z_peer(step):
        return {"imp": (lax.rem(z + step + nz, nz) * 2 + y) * 2 + c, "cre": g}

    y_peer = {"imp": (z * 2 + 1 - y) * 2 + c, "cre": g}
    core_peer = {"imp": q * 2 + 1 - c, "cre": g}

    own_rows = pl.ds(pl.multiple_of(c * rows, rows), rows)
    own_panel = pl.ds(pl.multiple_of(q * width, width), width)
    local = [
        pltpu.make_async_copy(price_hbm, pg_own.at[0], local_sem.at[0]),
        pltpu.make_async_copy(goal_hbm, pg_own.at[1], local_sem.at[1]),
        pltpu.make_async_copy(list_hbm, lists, local_sem.at[2]),
        pltpu.make_async_copy(weight_hbm, wl.at[c, pl.ds(0, own_tiles)], local_sem.at[3]),
        pltpu.make_async_copy(panel_hbm, panels.at[own_panel], local_sem.at[4]),
        pltpu.make_async_copy(imp_hbm, imps.at[own_rows], local_sem.at[5]),
    ]
    for copy in local:
        copy.start()

    barrier = pltpu.get_barrier_semaphore()
    for k in range(1, n_chip):
        pl.semaphore_signal(barrier, inc=1, device_id=chip_peer(k)[1], device_id_type=MESH)
    for k in range(1, n_x):
        pl.semaphore_signal(barrier, inc=1, device_id=cre_peer(k), device_id_type=MESH)

    for copy in local[:4]:
        copy.wait()
    pg[q] = jnp.concatenate([pg_own[0], pg_own[1]], axis=1)
    sub = lax.broadcasted_iota(jnp.int32, lists.shape, 0)
    lane = lax.broadcasted_iota(jnp.int32, lists.shape, 1)
    counts = jnp.zeros(lists.shape, jnp.int32)
    for t in range(own_tiles):
        counts = jnp.where(sub == t, count_ref[t], counts)
    wl[c, pl.ds(own_tiles, own_tiles)] = jnp.full((own_tiles, TILE), -1.0, F32)
    wl[c, pl.ds(own_tiles, own_tiles), pl.ds(0, lists.shape[1])] = jnp.where(
        lane < counts, lists[...].astype(F32), -1.0
    )

    pl.semaphore_wait(barrier, n_chip - 1 + n_x - 1)

    def panel_copy(src, slot, send, recv, peer):
        return pltpu.make_async_remote_copy(
            src_ref=src,
            dst_ref=panels.at[pl.ds(pl.multiple_of(slot * width, width), width)],
            send_sem=send,
            recv_sem=recv,
            device_id=peer,
            device_id_type=MESH,
        )

    sent = []

    def send(src, slot, recv, peer):
        copy = panel_copy(src, slot, panel_send.at[len(sent)], recv, peer)
        copy.start()
        sent.append(copy)
        return copy

    to_pair = send(panel_hbm, q, pair_sem.at[0], y_peer)
    to_right = {(0, 0): send(panel_hbm, q, right_sem.at[0, 0], z_peer(1))}
    to_left = {(0, 0): send(panel_hbm, q, left_sem.at[0, 0], z_peer(-1))}

    core_copies = [
        pltpu.make_async_remote_copy(
            src_ref=wl.at[c],
            dst_ref=wl.at[c],
            send_sem=core_send.at[0],
            recv_sem=core_recv.at[0],
            device_id=core_peer,
            device_id_type=MESH,
        ),
        pltpu.make_async_remote_copy(
            src_ref=imp_hbm,
            dst_ref=imps.at[own_rows],
            send_sem=core_send.at[1],
            recv_sem=core_recv.at[1],
            device_id=core_peer,
            device_id_type=MESH,
        ),
    ]
    for copy in core_copies:
        copy.start()
    pg_copies = []
    for k in range(1, n_chip):
        copy = pltpu.make_async_remote_copy(
            src_ref=pg.at[q],
            dst_ref=pg.at[q],
            send_sem=pg_send.at[k],
            recv_sem=pg_recv.at[q],
            device_id=chip_peer(k)[1],
            device_id_type=MESH,
        )
        copy.start()
        pg_copies.append(copy)

    core_copies[0].wait_recv()
    ids = lax.broadcasted_iota(jnp.int32, (n_chip, TILE), 0) + g * n_chip
    ids = ids.astype(F32)
    for t in range(tiles):
        row = wl[t // own_tiles, own_tiles + t % own_tiles : own_tiles + t % own_tiles + 1, :]
        hit = jnp.max(jnp.where(row == ids, 1.0, 0.0), axis=1, keepdims=True)
        bias[t] = jnp.broadcast_to(jnp.where(hit > 0.0, 0.0, NEG_FILL), (n_chip, TILE))

    for k in range(1, n_chip):
        other = lax.rem(q + k, n_chip)
        pltpu.make_async_remote_copy(
            src_ref=pg.at[q],
            dst_ref=pg.at[other],
            send_sem=pg_send.at[k],
            recv_sem=pg_recv.at[other],
            device_id=chip_peer(k)[1],
            device_id_type=MESH,
        ).wait_recv()
    low = lax.broadcasted_iota(jnp.int32, (1, TILE), 1) < width
    price_rows = []
    goal_rows = []
    for r in range(packed):
        even = pg[2 * r]
        odd = pg[2 * r + 1]
        price_rows.append(jnp.where(low, even, pltpu.roll(odd, width, 1)))
        goal_rows.append(jnp.where(low, pltpu.roll(even, width, 1), odd))
    price = jnp.concatenate(price_rows, axis=0)
    goal = jnp.concatenate(goal_rows, axis=0)

    def spread(value):
        v = jnp.exp(value)
        for r in range(packed):
            wide = jnp.broadcast_to(v[r : r + 1, :], (TILE, TILE))
            vcol[r * TILE : (r + 1) * TILE, :] = jnp.transpose(wide)
        return v

    v_lane = spread(price)

    other_shard = z * 2 + 1 - y
    to_pair_back = panel_copy(panel_hbm, other_shard, panel_send.at[0], pair_sem.at[0], y_peer)
    to_pair_back.wait_recv()

    def shard_ref(slot):
        return panels.at[pl.ds(pl.multiple_of(slot * width, width), width)]

    to_right[(0, 1)] = send(shard_ref(other_shard), other_shard, right_sem.at[0, 1], z_peer(1))
    to_left[(0, 1)] = send(shard_ref(other_shard), other_shard, left_sem.at[0, 1], z_peer(-1))

    local[4].wait()
    local[5].wait()
    core_copies[1].wait_recv()

    slab_rows = 2 * width

    def process(slabs):
        parts = []
        for zz in slabs:
            parts.append(panels[pl.ds(pl.multiple_of(zz * slab_rows, slab_rows), slab_rows), :])
        pan = parts[0] if len(parts) == 1 else jnp.concatenate(parts, axis=0)

        def body(t2, carry):
            x = imps[pl.ds(pl.multiple_of(t2 * 2 * TILE, 2 * TILE), 2 * TILE), :]
            aff = lax.dot_general(pan, x, (((1,), (1,)), ((), ())), preferred_element_type=F32)
            for n, zz in enumerate(slabs):
                for h in range(2):
                    qq = zz * 2 + h
                    at = pl.ds(pl.multiple_of(qq * width, width), width)
                    v = vcol[at, :]
                    for side in range(2):
                        t = t2 * 2 + side
                        first = n * slab_rows + h * width
                        a = aff[first : first + width, side * TILE : (side + 1) * TILE]
                        m = jnp.max(a, axis=0, keepdims=True)
                        e = jnp.exp2((a - m) * EXP2_SCALE)
                        kmat[t, at, :] = e
                        top[t, pl.ds(qq, 1), :] = TAU_INV * m
                        zsum[t, pl.ds(qq, 1), :] = jnp.sum(e * v, axis=0, keepdims=True)
            return carry

        lax.fori_loop(0, tiles // 2, body, 0)

    process([z])

    for d in range(1, half + 1):
        right_from = lax.rem(z - d + nz, nz)
        left_from = lax.rem(z + d, nz)
        for s in range(2):
            yy = y if s == 0 else 1 - y
            last = d == half
            if not last or s == 0:
                slot = right_from * 2 + yy
                panel_copy(
                    panel_hbm, slot, panel_send.at[0], right_sem.at[d - 1, s], z_peer(1)
                ).wait_recv()
                if d + 1 < half or (d + 1 == half and s == 0):
                    send(shard_ref(slot), slot, right_sem.at[d, s], z_peer(1))
            if not last or s == 1:
                slot = left_from * 2 + yy
                panel_copy(
                    panel_hbm, slot, panel_send.at[0], left_sem.at[d - 1, s], z_peer(-1)
                ).wait_recv()
                if d + 1 < half or (d + 1 == half and s == 1):
                    send(shard_ref(slot), slot, left_sem.at[d, s], z_peer(-1))
        process([right_from] if d == half else [right_from, left_from])

    def exchange_norms(phase):
        lse[phase, me_x] = mx_row[...] + jnp.log(zt_row[...])
        copies = []
        for k in range(1, n_x):
            copy = pltpu.make_async_remote_copy(
                src_ref=lse.at[phase, me_x],
                dst_ref=lse.at[phase, me_x],
                send_sem=x_send.at[phase, k],
                recv_sem=x_recv.at[phase, me_x],
                device_id=cre_peer(k),
                device_id_type=MESH,
            )
            copy.start()
            copies.append(copy)
        for k in range(1, n_x):
            other = lax.rem(me_x + k, n_x)
            pltpu.make_async_remote_copy(
                src_ref=lse.at[phase, me_x],
                dst_ref=lse.at[phase, other],
                send_sem=x_send.at[phase, k],
                recv_sem=x_recv.at[phase, other],
                device_id=cre_peer(k),
                device_id_type=MESH,
            ).wait_recv()
        most = lse[phase, 0]
        for k in range(1, n_x):
            most = jnp.maximum(most, lse[phase, k])
        total = jnp.exp(lse[phase, 0] - most)
        for k in range(1, n_x):
            total = total + jnp.exp(lse[phase, k] - most)
        norm = most + jnp.log(total)
        norms[0] = norm[:own_tiles]
        norms[1] = norm[own_tiles:]
        for t in range(tiles):
            w = wl[t // own_tiles, t % own_tiles : t % own_tiles + 1, :]
            rmat[t] = w * jnp.exp(top[t] + bias[t] - norm[t : t + 1, :])
        return copies

    def spends():
        ones = []
        for r in range(packed):

            def body(t, acc):
                k0 = kmat[t, r * TILE : r * TILE + width, :]
                k1 = kmat[t, r * TILE + width : (r + 1) * TILE, :]
                r0 = rmat[t, 2 * r : 2 * r + 1, :]
                r1 = rmat[t, 2 * r + 1 : 2 * r + 2, :]
                return (acc[0] + k0 * r0, acc[1] + k1 * r1)

            zero = jnp.zeros((width, TILE), F32)
            a0, a1 = lax.fori_loop(0, tiles, body, (zero, zero), unroll=4)
            ones.append(jnp.sum(jnp.transpose(jnp.concatenate([a0, a1], axis=0)), axis=0, keepdims=True))
        return ones

    for t in range(tiles):
        lim = top[t] + bias[t]
        m = jnp.max(lim, axis=0, keepdims=True)
        mx_row[t : t + 1, :] = m
        f = jnp.exp(lim - m)
        rmat[t] = f
        zt_row[t : t + 1, :] = jnp.sum(f * zsum[t], axis=0, keepdims=True)
    x_copies = exchange_norms(0)

    part1[q] = jnp.concatenate(spends(), axis=0) * v_lane
    y_copies = []
    for k in range(1, n_chip):
        copy = pltpu.make_async_remote_copy(
            src_ref=part1.at[q],
            dst_ref=part1.at[q],
            send_sem=y_send.at[0, k],
            recv_sem=y_recv.at[0, q],
            device_id=chip_peer(k)[1],
            device_id_type=MESH,
        )
        copy.start()
        y_copies.append(copy)
    for t in range(tiles):
        rmat[t] = jnp.exp(top[t] + bias[t] - mx_row[t : t + 1, :])
    for k in range(1, n_chip):
        other = lax.rem(q + k, n_chip)
        pltpu.make_async_remote_copy(
            src_ref=part1.at[q],
            dst_ref=part1.at[other],
            send_sem=y_send.at[0, k],
            recv_sem=y_recv.at[0, other],
            device_id=chip_peer(k)[1],
            device_id_type=MESH,
        ).wait_recv()
    spend = part1[0]
    for k in range(1, n_chip):
        spend = spend + part1[k]
    price = price + STEP_RATE * (jnp.log(goal) - jnp.log(spend + 0.25 * goal))
    v_lane = spread(price)

    def zbody(t, carry):
        acc = jnp.zeros((8, TILE), F32)
        for qq in range(n_chip):
            part = kmat[t, qq * width : (qq + 1) * width, :] * vcol[qq * width : (qq + 1) * width, :]
            acc = acc + jnp.sum(part.reshape(width // 8, 8, TILE), axis=0) * rmat[t, qq : qq + 1, :]
        zt_row[pl.ds(t, 1), :] = jnp.sum(acc, axis=0, keepdims=True)
        return carry

    lax.fori_loop(0, tiles, zbody, 0)
    x_copies += exchange_norms(1)

    for r, value in enumerate(spends()):
        part2[r] = value * v_lane[r : r + 1, :]
    for k in range(1, n_chip):
        other, peer = chip_peer(k)
        copy = pltpu.make_async_remote_copy(
            src_ref=part2.at[other // 2],
            dst_ref=got2.at[q],
            send_sem=y_send.at[1, k],
            recv_sem=y_recv.at[1, q],
            device_id=peer,
            device_id_type=MESH,
        )
        copy.start()
        y_copies.append(copy)
    got2[q] = part2[q // 2]
    norm_ref[...] = norms[c]
    for k in range(1, n_chip):
        other = lax.rem(q + k, n_chip)
        pltpu.make_async_remote_copy(
            src_ref=part2.at[0],
            dst_ref=got2.at[other],
            send_sem=y_send.at[1, k],
            recv_sem=y_recv.at[1, other],
            device_id=chip_peer(k)[1],
            device_id_type=MESH,
        ).wait_recv()
    spend = got2[0]
    for k in range(1, n_chip):
        spend = spend + got2[k]

    row = lax.broadcasted_iota(jnp.int32, (packed, TILE), 0)

    def own_half(value):
        return jnp.where(y == 0, value, pltpu.roll(value, width, 1))[:, :width]

    price_row = jnp.sum(jnp.where(row == z, price, 0.0), axis=0, keepdims=True)
    goal_row = jnp.sum(jnp.where(row == z, goal, 0.0), axis=0, keepdims=True)
    final = price_row + STEP_RATE * (jnp.log(goal_row) - jnp.log(spend + 0.25 * goal_row))
    spend_ref[...] = own_half(spend)
    new_price_ref[...] = own_half(final)

    for copy in sent + core_copies + pg_copies + x_copies + y_copies:
        copy.wait_send()


def solution(mesh):
    n_chip = mesh.shape["imp"] // 2
    n_cre = mesh.shape["cre"]
    half = n_chip // 4

    def step(impressions, panels, block_lists, block_counts, imp_weight, spend_goals, prices):
        rows, wide = impressions.shape
        width = panels.shape[1]
        own_tiles = rows // TILE
        tiles = 2 * own_tiles
        n_x = n_cre * 2
        creatives = n_chip * width
        any_spec = pl.BlockSpec(memory_space=pl.ANY)
        vmem = pl.BlockSpec(memory_space=pltpu.VMEM)
        dma = pltpu.SemaphoreType.DMA
        new_prices, spend, norms = pl.pallas_call(
            functools.partial(kernel, n_chip, n_cre),
            out_shape=(
                jax.ShapeDtypeStruct((1, width), F32),
                jax.ShapeDtypeStruct((1, width), F32),
                jax.ShapeDtypeStruct((own_tiles, TILE), F32),
            ),
            in_specs=[
                any_spec,
                any_spec,
                any_spec,
                pl.BlockSpec(memory_space=pltpu.SMEM),
                any_spec,
                any_spec,
                any_spec,
            ],
            out_specs=(vmem, vmem, vmem),
            scratch_shapes=[
                pltpu.VMEM((2 * rows, wide), jnp.bfloat16),
                pltpu.VMEM((creatives, wide), jnp.bfloat16),
                pltpu.VMEM((tiles, creatives, TILE), F32),
                pltpu.VMEM((tiles, n_chip, TILE), F32),
                pltpu.VMEM((tiles, n_chip, TILE), F32),
                pltpu.VMEM((tiles, n_chip, TILE), F32),
                pltpu.VMEM((tiles, n_chip, TILE), F32),
                pltpu.VMEM((creatives, TILE), F32),
                pltpu.VMEM((2, tiles, TILE), F32),
                pltpu.VMEM((own_tiles, block_lists.shape[1]), jnp.int32),
                pltpu.VMEM((2, 1, width), F32),
                pltpu.VMEM((n_chip, 1, TILE), F32),
                pltpu.VMEM((tiles, TILE), F32),
                pltpu.VMEM((tiles, TILE), F32),
                pltpu.VMEM((2, n_x, tiles, TILE), F32),
                pltpu.VMEM((2, own_tiles, TILE), F32),
                pltpu.VMEM((n_chip, n_chip // 2, TILE), F32),
                pltpu.VMEM((n_chip // 2, 1, TILE), F32),
                pltpu.VMEM((n_chip, 1, TILE), F32),
                dma((6,)),
                dma((4 * half + 1,)),
                dma((half, 2)),
                dma((half, 2)),
                dma((1,)),
                dma((n_chip,)),
                dma((n_chip,)),
                dma((2,)),
                dma((2,)),
                dma((2, n_x)),
                dma((2, n_x)),
                dma((2, n_chip)),
                dma((2, n_chip)),
            ],
            compiler_params=pltpu.CompilerParams(
                collective_id=0, has_side_effects=True, vmem_limit_bytes=40 << 20
            ),
        )(
            impressions,
            panels.reshape(width, wide),
            block_lists,
            block_counts,
            imp_weight.reshape(own_tiles, TILE),
            spend_goals,
            prices,
        )
        return new_prices, spend, norms.reshape(rows)

    return jax.shard_map(
        step,
        mesh=mesh,
        in_specs=(
            P("imp", None),
            P("cre", "imp", None),
            P("imp", None),
            P("imp"),
            P("imp"),
            P("cre", "imp"),
            P("cre", "imp"),
        ),
        out_specs=(P("cre", "imp"), P("cre", "imp"), P("imp")),
        check_vma=False,
    )
```

time: 429 us -> 65.8 us (0.15)
  blocking collectives: 337 us -> 0 us
  Pallas kernels: 0 us -> 59.4 us
  matrix products: 29.8 us -> 0 us
  between operations: 14.9 us -> 0.67 us
  local copies, waits for them, and re-layouts: 16.5 us -> 5.45 us
  loops' own time: 11 us -> 0 us
  waiting for transfers between devices: 10.4 us -> 0 us
  other arithmetic: 8.58 us -> 0 us
    psum x4 -> x0, blocking collectives: 171 us -> none  [the longest x2 146 us: shards(): summed = lax.psum(partial_spend, 'imp')]
    squeeze x2 -> x0, blocking collectives: 136 us -> none  [shards(): whole_prices = lax.all_gather(prices, 'imp', axis=1, tiled=True)[0]]
    pallas_call x0 -> x1, Pallas kernels: none -> 59.4 us  [step(): pl.pallas_call(functools.partial(kernel, n_chip, n_cre), out_shape=(jax.S...]
    dot_general x16 -> x0, matrix products: 29.8 us -> none  [scored(): lax.dot_general(impressions, panel_rows, (((1,), (1,)), ((), ())), prefer...]
    pmax x2 -> x0, blocking collectives: 29.1 us -> none  [shards(): merged_top = lax.pmax(row_top, 'cre')]
    another operation x4 -> x0, loops' own time: 11 us -> none  [sweep(): lax.scan(inner, running, jnp.arange(col_count // sub_width, dtype=jnp.int...]
    dynamic_slice x32 -> x0, local copies, waits for them, and re-layouts: 10.9 us -> none  [the longest x16 9.67 us: sweep(): lax.scan(inner, running, jnp.arange(col_count // sub_width, dtype=jnp.int...]
    all_gather x1 -> x0, waiting for transfers between devices: 9.76 us -> none  [shards(): lax.all_gather(panels, 'imp', axis=1, tiled=True)[0]]
  transfers between devices with their start and end apart: 1 -> 0, of which waited for: 1 -> 0; matrix products, arithmetic and copies ran while one was open for 1% -> 0% of each run, Pallas kernels for 0% -> 0%
where the time goes in v1:
time: 65.8 us; the launch traced here: 65.5 us
  Pallas kernels  59.4 us (90%)
  local copies, waits for them, and re-layouts  5.45 us (8%)
  between operations  0.67 us (1%)
    pallas_call x1, Pallas kernels, step(): pl.pallas_call(functools.partial(kernel, n_chip, n_cre), out_shape=(jax.S...  59.4 us
    unnamed x17, local copies, waits for them, and re-layouts  5.45 us

profile of v1, /device:TPU:1, one launch (start us, length us, event | category | flops | bytes accessed | tf_op | source)
XLA Modules:
  0.0 65.5 jit_solution(16488587559339631200)
XLA Ops:
  0.6 0.0 copy-start.4
  0.6 0.0 copy-start.5
  0.7 0.0 copy-start.6
  0.7 0.6 copy-done.4
  1.3 0.0 copy-done.5
  1.3 0.0 copy-done.6
  1.3 0.0 copy-start
  1.3 1.0 %copy-done = bf16[1024,256]{1,0:T(8,128)(2,1)S(1)} copy-done((bf16[1024,256]{1,0:T(8,128)(2,1)S(1)}, bf16[1024,256]{1,0:T(8,128)(2,1)}, u32[]{:S(2)}) %copy-start) | copy-done | bytes 524312
  2.4 0.0 copy-start.1
  2.4 0.8 %copy-done.1 = bf16[1,64,256]{2,1,0:T(8,128)(2,1)S(1)} copy-done((bf16[1,64,256]{2,1,0:T(8,128)(2,1)S(1)}, bf16[1,64,256]{2,1,0:T(8,128)(2,1)}, u32[]{:S(2)}) %copy-start.1) | copy-done | bytes 32792
  3.1 0.0 copy-start.2
  3.1 0.7 %copy-done.2 = s32[8,16]{1,0:T(8,128)S(1)} copy-done((s32[8,16]{1,0:T(8,128)S(1)}, s32[8,16]{1,0:T(8,128)}, u32[]{:S(2)}) %copy-start.2) | copy-done | bytes 536
  3.8 0.0 copy-start.3
  3.8 0.7 %copy-done.3 = f32[1024]{0:T(1024)S(1)} copy-done((f32[1024]{0:T(1024)S(1)}, f32[1024]{0:T(1024)}, u32[]{:S(2)}) %copy-start.3) | copy-done | bytes 4120
  4.5 59.4 %shard_map.94 = (f32[1,64]{1,0:T(1,128)S(1)}, f32[1,64]{1,0:T(1,128)S(1)}, f32[8,128]{1,0:T(8,128)S(1)}) custom-call(bf16[1024,256]{1,0:T(8,128)(2,1)S(1)} %copy-done, bf16[64,256]{1,0:T(8,128)(2,1)S(1)} %bitcast.3, s32[8,16]{1,0:T(8,128)S(1)} %copy-done.2, s32[8]{0:T(128)S(1)} %copy-done.4, f32[8,128]{1,0:T(8,128)S(1)} %bitcast.4, f32[1,64]{1,0:T(1,128)S(1)} %copy-done.5, ...), custom_call_target="tpu_custom_call" | custom-call | tf_op jit(solution)/shard_map/pallas_call | solution.py:455
  63.9 0.5 copy.13
  64.4 0.5 copy.14
  64.9 0.6 copy.15
Async XLA Ops:
  0.6 0.7 %copy-start.4 = (s32[8]{0:T(128)S(1)}, s32[8]{0:T(128)}, u32[]{:S(2)}) copy-start(s32[8]{0:T(128)} %count_ref.1) | copy-start | bytes 100
  0.6 0.7 %copy-start.5 = (f32[1,64]{1,0:T(1,128)S(1)}, f32[1,64]{1,0:T(1,128)}, u32[]{:S(2)}) copy-start(f32[1,64]{1,0:T(1,128)} %goal_hbm.1) | copy-start | bytes 772
  0.7 0.7 %copy-start.6 = (f32[1,64]{1,0:T(1,128)S(1)}, f32[1,64]{1,0:T(1,128)}, u32[]{:S(2)}) copy-start(f32[1,64]{1,0:T(1,128)} %price_hbm.1) | copy-start | bytes 772
  1.3 1.0 %copy-start = (bf16[1024,256]{1,0:T(8,128)(2,1)S(1)}, bf16[1024,256]{1,0:T(8,128)(2,1)}, u32[]{:S(2)}) copy-start(bf16[1024,256]{1,0:T(8,128)(2,1)} %imp_hbm.1) | copy-start | bytes 1572868
  2.4 0.8 %copy-start.1 = (bf16[1,64,256]{2,1,0:T(8,128)(2,1)S(1)}, bf16[1,64,256]{2,1,0:T(8,128)(2,1)}, u32[]{:S(2)}) copy-start(bf16[1,64,256]{2,1,0:T(8,128)(2,1)} %param.8) | copy-start | bytes 98308
  3.1 0.7 %copy-start.2 = (s32[8,16]{1,0:T(8,128)S(1)}, s32[8,16]{1,0:T(8,128)}, u32[]{:S(2)}) copy-start(s32[8,16]{1,0:T(8,128)} %list_hbm.1) | copy-start | bytes 1540
  3.8 0.7 %copy-start.3 = (f32[1024]{0:T(1024)S(1)}, f32[1024]{0:T(1024)}, u32[]{:S(2)}) copy-start(f32[1024]{0:T(1024)} %param.11) | copy-start | bytes 12292

commit v2 on v1

--- a/solution.py
+++ b/solution.py
@@ -51,9 +51,7 @@
     got2,
     local_sem,
     panel_send,
-    right_sem,
-    left_sem,
-    pair_sem,
+    panel_recv,
     pg_send,
     pg_recv,
     core_send,
@@ -79,42 +77,110 @@
     own_tiles = tiles // 2
     packed = n_chip // 2
 
-    def chip_peer(k):
-        other = lax.rem(q + k, n_chip)
-        return other, {"imp": other * 2 + c, "cre": g}
+    mirror = g + 1 - 2 * lax.rem(g, 2)
+
+    def plane(step):
+        return lax.rem(z + step + nz, nz)
+
+    def slot_of(step, dy):
+        return plane(step) * 2 + (y if dy == 0 else 1 - y)
+
+    def at(step, dy):
+        return {"imp": slot_of(step, dy) * 2 + c, "cre": g if dy == 0 else mirror}
+
+    chips = [(half, 1), (half, 0)]
+    for d in range(half - 1, 0, -1):
+        chips += [(d, 1), (-d, 1), (d, 0), (-d, 0)]
+    chips += [(0, 1)]
 
     def cre_peer(k):
         other = lax.rem(me_x + k, n_x)
         return {"imp": q * 2 + lax.rem(other, 2), "cre": other // 2}
 
-    def z_peer(step):
-        return {"imp": (lax.rem(z + step + nz, nz) * 2 + y) * 2 + c, "cre": g}
-
-    y_peer = {"imp": (z * 2 + 1 - y) * 2 + c, "cre": g}
+    far_first = sorted(range(1, n_x), key=lambda k: -min(k, n_x - k))
     core_peer = {"imp": q * 2 + 1 - c, "cre": g}
 
+    barrier = pltpu.get_barrier_semaphore()
+    for step, dy in chips:
+        pl.semaphore_signal(barrier, inc=1, device_id=at(step, dy), device_id_type=MESH)
+    for k in far_first:
+        pl.semaphore_signal(barrier, inc=1, device_id=cre_peer(k), device_id_type=MESH)
+
     own_rows = pl.ds(pl.multiple_of(c * rows, rows), rows)
-    own_panel = pl.ds(pl.multiple_of(q * width, width), width)
+
+    def shard_ref(slot):
+        return panels.at[pl.ds(pl.multiple_of(slot * width, width), width)]
+
     local = [
         pltpu.make_async_copy(price_hbm, pg_own.at[0], local_sem.at[0]),
         pltpu.make_async_copy(goal_hbm, pg_own.at[1], local_sem.at[1]),
         pltpu.make_async_copy(list_hbm, lists, local_sem.at[2]),
         pltpu.make_async_copy(weight_hbm, wl.at[c, pl.ds(0, own_tiles)], local_sem.at[3]),
-        pltpu.make_async_copy(panel_hbm, panels.at[own_panel], local_sem.at[4]),
+        pltpu.make_async_copy(panel_hbm, shard_ref(q), local_sem.at[4]),
         pltpu.make_async_copy(imp_hbm, imps.at[own_rows], local_sem.at[5]),
     ]
     for copy in local:
         copy.start()
 
-    barrier = pltpu.get_barrier_semaphore()
-    for k in range(1, n_chip):
-        pl.semaphore_signal(barrier, inc=1, device_id=chip_peer(k)[1], device_id_type=MESH)
-    for k in range(1, n_x):
-        pl.semaphore_signal(barrier, inc=1, device_id=cre_peer(k), device_id_type=MESH)
-
-    for copy in local[:4]:
+    pl.semaphore_wait(barrier, n_chip - 1 + n_x - 1)
+
+    sent = []
+
+    def panel_copy(src, slot, peer, n=0):
+        return pltpu.make_async_remote_copy(
+            src_ref=src,
+            dst_ref=shard_ref(slot),
+            send_sem=panel_send.at[n],
+            recv_sem=panel_recv.at[slot],
+            device_id=peer,
+            device_id_type=MESH,
+        )
+
+    def send(src, slot, peer):
+        copy = panel_copy(src, slot, peer, len(sent))
+        copy.start()
+        sent.append(copy)
+
+    def arrived(step, dy):
+        panel_copy(panel_hbm, slot_of(step, dy), at(0, 1)).wait_recv()
+
+    for step in (2, -2, 1, -1):
+        for dy in (1, 0):
+            send(panel_hbm, q, at(step, dy))
+    send(panel_hbm, q, at(0, 1))
+
+    imp_copy = pltpu.make_async_remote_copy(
+        src_ref=imp_hbm,
+        dst_ref=imps.at[own_rows],
+        send_sem=core_send.at[1],
+        recv_sem=core_recv.at[1],
+        device_id=core_peer,
+        device_id_type=MESH,
+    )
+    imp_copy.start()
+
+    for copy in local[:2]:
         copy.wait()
     pg[q] = jnp.concatenate([pg_own[0], pg_own[1]], axis=1)
+    pg_copies = []
+
+    def pg_copy(k, slot):
+        return pltpu.make_async_remote_copy(
+            src_ref=pg.at[q],
+            dst_ref=pg.at[slot],
+            send_sem=pg_send.at[k],
+            recv_sem=pg_recv.at[slot],
+            device_id=at(*chips[k]),
+            device_id_type=MESH,
+        )
+
+    for k in range(n_chip - 1):
+        copy = pg_copy(k, q)
+        copy.start()
+        pg_copies.append(copy)
+
+    for copy in local[2:4]:
+        copy.wait()
     sub = lax.broadcasted_iota(jnp.int32, lists.shape, 0)
     lane = lax.broadcasted_iota(jnp.int32, lists.shape, 1)
     counts = jnp.zeros(lists.shape, jnp.int32)
@@ -124,82 +190,37 @@
     wl[c, pl.ds(own_tiles, own_tiles), pl.ds(0, lists.shape[1])] = jnp.where(
         lane < counts, lists[...].astype(F32), -1.0
     )
-
-    pl.semaphore_wait(barrier, n_chip - 1 + n_x - 1)
-
-    def panel_copy(src, slot, send, recv, peer):
-        return pltpu.make_async_remote_copy(
-            src_ref=src,
-            dst_ref=panels.at[pl.ds(pl.multiple_of(slot * width, width), width)],
-            send_sem=send,
-            recv_sem=recv,
-            device_id=peer,
-            device_id_type=MESH,
-        )
-
-    sent = []
-
-    def send(src, slot, recv, peer):
-        copy = panel_copy(src, slot, panel_send.at[len(sent)], recv, peer)
-        copy.start()
-        sent.append(copy)
-        return copy
-
-    to_pair = send(panel_hbm, q, pair_sem.at[0], y_peer)
-    to_right = {(0, 0): send(panel_hbm, q, right_sem.at[0, 0], z_peer(1))}
-    to_left = {(0, 0): send(panel_hbm, q, left_sem.at[0, 0], z_peer(-1))}
-
-    core_copies = [
-        pltpu.make_async_remote_copy(
-            src_ref=wl.at[c],
-            dst_ref=wl.at[c],
-            send_sem=core_send.at[0],
-            recv_sem=core_recv.at[0],
-            device_id=core_peer,
-            device_id_type=MESH,
-        ),
-        pltpu.make_async_remote_copy(
-            src_ref=imp_hbm,
-            dst_ref=imps.at[own_rows],
-            send_sem=core_send.at[1],
-            recv_sem=core_recv.at[1],
-            device_id=core_peer,
-            device_id_type=MESH,
-        ),
-    ]
-    for copy in core_copies:
-        copy.start()
-    pg_copies = []
-    for k in range(1, n_chip):
-        copy = pltpu.make_async_remote_copy(
-            src_ref=pg.at[q],
-            dst_ref=pg.at[q],
-            send_sem=pg_send.at[k],
-            recv_sem=pg_recv.at[q],
-            device_id=chip_peer(k)[1],
-            device_id_type=MESH,
-        )
-        copy.start()
-        pg_copies.append(copy)
-
-    core_copies[0].wait_recv()
-    ids = lax.broadcasted_iota(jnp.int32, (n_chip, TILE), 0) + g * n_chip
+    wl_copy = pltpu.make_async_remote_copy(
+        src_ref=wl.at[c],
+        dst_ref=wl.at[c],
+        send_sem=core_send.at[0],
+        recv_sem=core_recv.at[0],
+        device_id=core_peer,
+        device_id_type=MESH,
+    )
+    wl_copy.start()
+    core_copies = [wl_copy, imp_copy]
+
+    wl_copy.wait_recv()
+    ids = lax.broadcasted_iota(jnp.int32, (n_chip, TILE), 0)
+    ids = ids + jnp.where(lax.rem(ids, 2) == y, g, mirror) * n_chip
     ids = ids.astype(F32)
     for t in range(tiles):
         row = wl[t // own_tiles, own_tiles + t % own_tiles : own_tiles + t % own_tiles + 1, :]
         hit = jnp.max(jnp.where(row == ids, 1.0, 0.0), axis=1, keepdims=True)
         bias[t] = jnp.broadcast_to(jnp.where(hit > 0.0, 0.0, NEG_FILL), (n_chip, TILE))
 
-    for k in range(1, n_chip):
-        other = lax.rem(q + k, n_chip)
-        pltpu.make_async_remote_copy(
-            src_ref=pg.at[q],
-            dst_ref=pg.at[other],
-            send_sem=pg_send.at[k],
-            recv_sem=pg_recv.at[other],
-            device_id=chip_peer(k)[1],
-            device_id_type=MESH,
-        ).wait_recv()
+    for sign in (1, -1):
+        for s in range(2):
+            dy = s if sign == 1 else 1 - s
+            slot = slot_of(-2 * sign, dy)
+            arrived(-2 * sign, dy)
+            if s == 0:
+                send(shard_ref(slot), slot, at(2 * sign, 0))
+            send(shard_ref(slot), slot, at(sign, 0))
+
+    for k in range(n_chip - 1):
+        pg_copy(k, slot_of(*chips[k])).wait_recv()
     low = lax.broadcasted_iota(jnp.int32, (1, TILE), 1) < width
     price_rows = []
     goal_rows = []
@@ -220,20 +241,6 @@
 
     v_lane = spread(price)
 
-    other_shard = z * 2 + 1 - y
-    to_pair_back = panel_copy(panel_hbm, other_shard, panel_send.at[0], pair_sem.at[0], y_peer)
-    to_pair_back.wait_recv()
-
-    def shard_ref(slot):
-        return panels.at[pl.ds(pl.multiple_of(slot * width, width), width)]
-
-    to_right[(0, 1)] = send(shard_ref(other_shard), other_shard, right_sem.at[0, 1], z_peer(1))
-    to_left[(0, 1)] = send(shard_ref(other_shard), other_shard, left_sem.at[0, 1], z_peer(-1))
-
-    local[4].wait()
-    local[5].wait()
-    core_copies[1].wait_recv()
-
     slab_rows = 2 * width
 
     def process(slabs):
@@ -248,49 +255,40 @@
             for n, zz in enumerate(slabs):
                 for h in range(2):
                     qq = zz * 2 + h
-                    at = pl.ds(pl.multiple_of(qq * width, width), width)
-                    v = vcol[at, :]
+                    place = pl.ds(pl.multiple_of(qq * width, width), width)
+                    v = vcol[place, :]
                     for side in range(2):
                         t = t2 * 2 + side
                         first = n * slab_rows + h * width
                         a = aff[first : first + width, side * TILE : (side + 1) * TILE]
                         m = jnp.max(a, axis=0, keepdims=True)
                         e = jnp.exp2((a - m) * EXP2_SCALE)
-                        kmat[t, at, :] = e
+                        kmat[t, place, :] = e
                         top[t, pl.ds(qq, 1), :] = TAU_INV * m
                         zsum[t, pl.ds(qq, 1), :] = jnp.sum(e * v, axis=0, keepdims=True)
             return carry
 
-        lax.fori_loop(0, tiles // 2, body, 0)
-
+        lax.fori_loop(0, tiles // 2, body, 0, unroll=8)
+
+    for copy in local[4:]:
+        copy.wait()
+    imp_copy.wait_recv()
+    arrived(0, 1)
     process([z])
-
-    for d in range(1, half + 1):
-        right_from = lax.rem(z - d + nz, nz)
-        left_from = lax.rem(z + d, nz)
-        for s in range(2):
-            yy = y if s == 0 else 1 - y
-            last = d == half
-            if not last or s == 0:
-                slot = right_from * 2 + yy
-                panel_copy(
-                    panel_hbm, slot, panel_send.at[0], right_sem.at[d - 1, s], z_peer(1)
-                ).wait_recv()
-                if d + 1 < half or (d + 1 == half and s == 0):
-                    send(shard_ref(slot), slot, right_sem.at[d, s], z_peer(1))
-            if not last or s == 1:
-                slot = left_from * 2 + yy
-                panel_copy(
-                    panel_hbm, slot, panel_send.at[0], left_sem.at[d - 1, s], z_peer(-1)
-                ).wait_recv()
-                if d + 1 < half or (d + 1 == half and s == 1):
-                    send(shard_ref(slot), slot, left_sem.at[d, s], z_peer(-1))
-        process([right_from] if d == half else [right_from, left_from])
+    for d in range(1, half):
+        for step in (d, -d):
+            for dy in range(2):
+                if d != 2:
+                    arrived(step, dy)
+        process([plane(d), plane(-d)])
+    for dy in range(2):
+        arrived(half, dy)
+    process([plane(half)])
 
     def exchange_norms(phase):
         lse[phase, me_x] = mx_row[...] + jnp.log(zt_row[...])
         copies = []
-        for k in range(1, n_x):
+        for k in far_first:
             copy = pltpu.make_async_remote_copy(
                 src_ref=lse.at[phase, me_x],
                 dst_ref=lse.at[phase, me_x],
@@ -352,27 +350,27 @@
 
     part1[q] = jnp.concatenate(spends(), axis=0) * v_lane
     y_copies = []
-    for k in range(1, n_chip):
+    for k in range(n_chip - 1):
         copy = pltpu.make_async_remote_copy(
             src_ref=part1.at[q],
             dst_ref=part1.at[q],
             send_sem=y_send.at[0, k],
             recv_sem=y_recv.at[0, q],
-            device_id=chip_peer(k)[1],
+            device_id=at(*chips[k]),
             device_id_type=MESH,
         )
         copy.start()
         y_copies.append(copy)
     for t in range(tiles):
         rmat[t] = jnp.exp(top[t] + bias[t] - mx_row[t : t + 1, :])
-    for k in range(1, n_chip):
-        other = lax.rem(q + k, n_chip)
+    for k in range(n_chip - 1):
+        other = slot_of(*chips[k])
         pltpu.make_async_remote_copy(
             src_ref=part1.at[q],
             dst_ref=part1.at[other],
             send_sem=y_send.at[0, k],
             recv_sem=y_recv.at[0, other],
-            device_id=chip_peer(k)[1],
+            device_id=at(*chips[k]),
             device_id_type=MESH,
         ).wait_recv()
     spend = part1[0]
@@ -394,8 +392,8 @@
 
     for r, value in enumerate(spends()):
         part2[r] = value * v_lane[r : r + 1, :]
-    for k in range(1, n_chip):
-        other, peer = chip_peer(k)
+    for k in range(n_chip - 1):
+        other, peer = slot_of(*chips[k]), at(*chips[k])
         copy = pltpu.make_async_remote_copy(
             src_ref=part2.at[other // 2],
             dst_ref=got2.at[q],
@@ -408,14 +406,14 @@
         y_copies.append(copy)
     got2[q] = part2[q // 2]
     norm_ref[...] = norms[c]
-    for k in range(1, n_chip):
-        other = lax.rem(q + k, n_chip)
+    for k in range(n_chip - 1):
+        other = slot_of(*chips[k])
         pltpu.make_async_remote_copy(
             src_ref=part2.at[0],
             dst_ref=got2.at[other],
             send_sem=y_send.at[1, k],
             recv_sem=y_recv.at[1, other],
-            device_id=chip_peer(k)[1],
+            device_id=at(*chips[k]),
             device_id_type=MESH,
         ).wait_recv()
     spend = got2[0]
@@ -490,10 +488,8 @@
                 pltpu.VMEM((n_chip // 2, 1, TILE), F32),
                 pltpu.VMEM((n_chip, 1, TILE), F32),
                 dma((6,)),
-                dma((4 * half + 1,)),
-                dma((half, 2)),
-                dma((half, 2)),
-                dma((1,)),
+                dma((n_chip - 1,)),
+                dma((n_chip,)),
                 dma((n_chip,)),
                 dma((n_chip,)),
                 dma((2,)),
@@ -504,7 +500,7 @@
                 dma((2, n_chip)),
             ],
             compiler_params=pltpu.CompilerParams(
-                collective_id=0, has_side_effects=True, vmem_limit_bytes=40 << 20
+                collective_id=0, has_side_effects=True, vmem_limit_bytes=63 << 20
             ),
         )(
             impressions,

time: 65.8 us -> 53 us (0.81)
  Pallas kernels: 59.4 us -> 49.9 us
  local copies, waits for them, and re-layouts: 5.45 us -> 2.3 us
    pallas_call x1, Pallas kernels: 59.4 us -> 49.9 us  [step(): pl.pallas_call(functools.partial(kernel, n_chip, n_cre), out_shape=(jax.S...]
    unnamed x17 -> x9, local copies, waits for them, and re-layouts: 5.45 us -> 2.3 us
where the time goes in v2:
time: 53 us; the launch traced here: 52.9 us
  Pallas kernels  49.9 us (94%)
  local copies, waits for them, and re-layouts  2.3 us (4%)
  between operations  0.66 us (1%)
    pallas_call x1, Pallas kernels, step(): pl.pallas_call(functools.partial(kernel, n_chip, n_cre), out_shape=(jax.S...  49.9 us
    unnamed x9, local copies, waits for them, and re-layouts  2.3 us

profile of v2, /device:TPU:1, one launch (start us, length us, event | category | flops | bytes accessed | tf_op | source)
XLA Modules:
  0.0 52.9 jit_solution(8367616224368732445)
XLA Ops:
  0.6 49.9 %shard_map.94 = (f32[1,64]{1,0:T(1,128)}, f32[1,64]{1,0:T(1,128)}, f32[8,128]{1,0:T(8,128)}) custom-call(bf16[1024,256]{1,0:T(8,128)(2,1)} %imp_hbm.1, bf16[64,256]{1,0:T(8,128)(2,1)} %bitcast.3, s32[8,16]{1,0:T(8,128)} %list_hbm.1, s32[8]{0:T(128)} %count_ref.1, f32[8,128]{1,0:T(8,128)} %bitcast.4, f32[1,64]{1,0:T(1,128)} %goal_hbm.1, f32[1,64]{1,0:T(1,128)} %price_hbm.1), custom_call_target="tpu_custom_call" | custom-call | tf_op jit(solution)/shard_map/pallas_call | solution.py:453
  50.6 0.0 copy-start.2
  50.6 0.0 copy-start
  50.6 0.6 %copy-done.2 = f32[1,64]{1,0:T(1,128)S(1)} copy-done((f32[1,64]{1,0:T(1,128)S(1)}, f32[1,64]{1,0:T(1,128)}, u32[]{:S(2)}) %copy-start.2) | copy-done | bytes 280
  51.2 0.0 copy-start.1
  51.2 0.5 copy.13
  51.7 0.1 copy-done.1
  51.8 0.5 copy.14
  52.3 0.0 copy-done
  52.3 0.6 %copy.15 = f32[1024]{0:T(1024)} copy(f32[1024]{0:T(1024)S(1)} %bitcast.5) | data formatting | bytes 8192
Async XLA Ops:
  50.6 0.6 %copy-start.2 = (f32[1,64]{1,0:T(1,128)S(1)}, f32[1,64]{1,0:T(1,128)}, u32[]{:S(2)}) copy-start(f32[1,64]{1,0:T(1,128)} %get-tuple-element.12) | copy-start | bytes 772
  50.6 1.7 %copy-start = (f32[8,128]{1,0:T(8,128)S(1)}, f32[8,128]{1,0:T(8,128)}, u32[]{:S(2)}) copy-start(f32[8,128]{1,0:T(8,128)} %get-tuple-element.8) | copy-start | bytes 12292
  51.2 0.6 %copy-start.1 = (f32[1,64]{1,0:T(1,128)S(1)}, f32[1,64]{1,0:T(1,128)}, u32[]{:S(2)}) copy-start(f32[1,64]{1,0:T(1,128)} %get-tuple-element.13) | copy-start | bytes 772

commit v3 on v2

--- a/solution.py
+++ b/solution.py
@@ -27,7 +27,6 @@
     weight_hbm,
     goal_hbm,
     price_hbm,
-    new_price_ref,
     spend_ref,
     norm_ref,
     imps,
@@ -36,7 +35,8 @@
     top,
     zsum,
     bias,
-    rmat,
+    factor,
+    grow,
     vcol,
     wl,
     lists,
@@ -101,7 +101,8 @@
     core_peer = {"imp": q * 2 + 1 - c, "cre": g}
 
     barrier = pltpu.get_barrier_semaphore()
-    for step, dy in chips:
+    near = [(step, dy) for step, dy in chips if abs(step) <= 2]
+    for step, dy in near:
         pl.semaphore_signal(barrier, inc=1, device_id=at(step, dy), device_id_type=MESH)
     for k in far_first:
         pl.semaphore_signal(barrier, inc=1, device_id=cre_peer(k), device_id_type=MESH)
@@ -122,7 +123,33 @@
     for copy in local:
         copy.start()
 
-    pl.semaphore_wait(barrier, n_chip - 1 + n_x - 1)
+    for copy in local[:2]:
+        copy.wait()
+    pg[q] = jnp.concatenate([pg_own[0], pg_own[1]], axis=1)
+    pl.semaphore_wait(barrier, len(near) + n_x - 1)
+
+    pg_copies = []
+
+    def pg_copy(slot, peer, n=0):
+        return pltpu.make_async_remote_copy(
+            src_ref=pg.at[slot],
+            dst_ref=pg.at[slot],
+            send_sem=pg_send.at[n],
+            recv_sem=pg_recv.at[slot],
+            device_id=peer,
+            device_id_type=MESH,
+        )
+
+    def pg_put(slot, peer):
+        copy = pg_copy(slot, peer, len(pg_copies))
+        copy.start()
+        pg_copies.append(copy)
+
+    def pg_arrived(step, dy):
+        pg_copy(slot_of(step, dy), at(0, 1)).wait_recv()
+
+    for step, dy in near:
+        pg_put(q, at(step, dy))
 
     sent = []
 
@@ -158,26 +185,6 @@
         device_id_type=MESH,
     )
     imp_copy.start()
-
-    for copy in local[:2]:
-        copy.wait()
-    pg[q] = jnp.concatenate([pg_own[0], pg_own[1]], axis=1)
-    pg_copies = []
-
-    def pg_copy(k, slot):
-        return pltpu.make_async_remote_copy(
-            src_ref=pg.at[q],
-            dst_ref=pg.at[slot],
-            send_sem=pg_send.at[k],
-            recv_sem=pg_recv.at[slot],
-            device_id=at(*chips[k]),
-            device_id_type=MESH,
-        )
-
-    for k in range(n_chip - 1):
-        copy = pg_copy(k, q)
-        copy.start()
-        pg_copies.append(copy)
 
     for copy in local[2:4]:
         copy.wait()
@@ -208,20 +215,91 @@
     for t in range(tiles):
         row = wl[t // own_tiles, own_tiles + t % own_tiles : own_tiles + t % own_tiles + 1, :]
         hit = jnp.max(jnp.where(row == ids, 1.0, 0.0), axis=1, keepdims=True)
-        bias[t] = jnp.broadcast_to(jnp.where(hit > 0.0, 0.0, NEG_FILL), (n_chip, TILE))
+        level = jnp.broadcast_to(jnp.where(hit > 0.0, 0.0, NEG_FILL), (n_chip, TILE))
+        for b in range(n_chip):
+            bias[t, b] = jnp.broadcast_to(level[b : b + 1, :], (8, TILE))
 
     for sign in (1, -1):
         for s in range(2):
             dy = s if sign == 1 else 1 - s
             slot = slot_of(-2 * sign, dy)
+            pg_arrived(-2 * sign, dy)
+            if s == 0:
+                pg_put(slot, at(2 * sign, 0))
+            pg_put(slot, at(sign, 0))
             arrived(-2 * sign, dy)
             if s == 0:
                 send(shard_ref(slot), slot, at(2 * sign, 0))
             send(shard_ref(slot), slot, at(sign, 0))
 
-    for k in range(n_chip - 1):
-        pg_copy(k, slot_of(*chips[k])).wait_recv()
     low = lax.broadcasted_iota(jnp.int32, (1, TILE), 1) < width
+    def spread(value):
+        v = jnp.exp(value)
+        for r in range(packed):
+            wide = jnp.broadcast_to(v[r : r + 1, :], (TILE, TILE))
+            vcol[r * TILE : (r + 1) * TILE, :] = jnp.transpose(wide)
+        return v
+
+    def spread_slab(zz):
+        row = jnp.where(low, pg[2 * zz], pltpu.roll(pg[2 * zz + 1], width, 1))
+        wide = jnp.broadcast_to(jnp.exp(row), (TILE, TILE))
+        vcol[pl.ds(pl.multiple_of(zz * TILE, TILE), TILE), :] = jnp.transpose(wide)
+
+    slab_rows = 2 * width
+
+    def process(slabs):
+        parts = []
+        for zz in slabs:
+            parts.append(panels[pl.ds(pl.multiple_of(zz * slab_rows, slab_rows), slab_rows), :])
+        pan = parts[0] if len(parts) == 1 else jnp.concatenate(parts, axis=0)
+
+        def body(t2, carry):
+            x = imps[pl.ds(pl.multiple_of(t2 * 2 * TILE, 2 * TILE), 2 * TILE), :]
+            aff = lax.dot_general(pan, x, (((1,), (1,)), ((), ())), preferred_element_type=F32)
+            for n, zz in enumerate(slabs):
+                for h in range(2):
+                    qq = zz * 2 + h
+                    place = pl.ds(pl.multiple_of(qq * width, width), width)
+                    v = vcol[place, :].reshape(width // 8, 8, TILE)
+                    for side in range(2):
+                        t = t2 * 2 + side
+                        first = n * slab_rows + h * width
+                        a = aff[first : first + width, side * TILE : (side + 1) * TILE]
+                        a = a.reshape(width // 8, 8, TILE)
+                        m = jnp.max(a, axis=0)
+                        e = jnp.exp2((a - m) * EXP2_SCALE)
+                        kmat[t, place, :] = e.reshape(width, TILE)
+                        top[t, qq] = TAU_INV * m + bias[t, qq]
+                        zsum[t, qq] = jnp.sum(e * v, axis=0)
+            return carry
+
+        lax.fori_loop(0, tiles // 2, body, 0, unroll=8)
+
+    for copy in local[4:]:
+        copy.wait()
+    imp_copy.wait_recv()
+    pg_arrived(0, 1)
+    spread_slab(z)
+    arrived(0, 1)
+    process([z])
+    for d in range(1, half):
+        for step in (d, -d):
+            for dy in range(2):
+                if d != 2:
+                    pg_arrived(step, dy)
+            spread_slab(plane(step))
+        for step in (d, -d):
+            for dy in range(2):
+                if d != 2:
+                    arrived(step, dy)
+        process([plane(d), plane(-d)])
+    for dy in range(2):
+        pg_arrived(half, dy)
+    spread_slab(plane(half))
+    for dy in range(2):
+        arrived(half, dy)
+    process([plane(half)])
+
     price_rows = []
     goal_rows = []
     for r in range(packed):
@@ -232,58 +310,7 @@
     price = jnp.concatenate(price_rows, axis=0)
     goal = jnp.concatenate(goal_rows, axis=0)
 
-    def spread(value):
-        v = jnp.exp(value)
-        for r in range(packed):
-            wide = jnp.broadcast_to(v[r : r + 1, :], (TILE, TILE))
-            vcol[r * TILE : (r + 1) * TILE, :] = jnp.transpose(wide)
-        return v
-
-    v_lane = spread(price)
-
-    slab_rows = 2 * width
-
-    def process(slabs):
-        parts = []
-        for zz in slabs:
-            parts.append(panels[pl.ds(pl.multiple_of(zz * slab_rows, slab_rows), slab_rows), :])
-        pan = parts[0] if len(parts) == 1 else jnp.concatenate(parts, axis=0)
-
-        def body(t2, carry):
-            x = imps[pl.ds(pl.multiple_of(t2 * 2 * TILE, 2 * TILE), 2 * TILE), :]
-            aff = lax.dot_general(pan, x, (((1,), (1,)), ((), ())), preferred_element_type=F32)
-            for n, zz in enumerate(slabs):
-                for h in range(2):
-                    qq = zz * 2 + h
-                    place = pl.ds(pl.multiple_of(qq * width, width), width)
-                    v = vcol[place, :]
-                    for side in range(2):
-                        t = t2 * 2 + side
-                        first = n * slab_rows + h * width
-                        a = aff[first : first + width, side * TILE : (side + 1) * TILE]
-                        m = jnp.max(a, axis=0, keepdims=True)
-                        e = jnp.exp2((a - m) * EXP2_SCALE)
-                        kmat[t, place, :] = e
-                        top[t, pl.ds(qq, 1), :] = TAU_INV * m
-                        zsum[t, pl.ds(qq, 1), :] = jnp.sum(e * v, axis=0, keepdims=True)
-            return carry
-
-        lax.fori_loop(0, tiles // 2, body, 0, unroll=8)
-
-    for copy in local[4:]:
-        copy.wait()
-    imp_copy.wait_recv()
-    arrived(0, 1)
-    process([z])
-    for d in range(1, half):
-        for step in (d, -d):
-            for dy in range(2):
-                if d != 2:
-                    arrived(step, dy)
-        process([plane(d), plane(-d)])
-    for dy in range(2):
-        arrived(half, dy)
-    process([plane(half)])
+    v_lane = jnp.exp(price)
 
     def exchange_norms(phase):
         lse[phase, me_x] = mx_row[...] + jnp.log(zt_row[...])
@@ -318,9 +345,10 @@
         norm = most + jnp.log(total)
         norms[0] = norm[:own_tiles]
         norms[1] = norm[own_tiles:]
+        weight = jnp.concatenate([wl[0, :own_tiles], wl[1, :own_tiles]], axis=0)
+        gain = weight * jnp.exp(mx_row[...] - norm)
         for t in range(tiles):
-            w = wl[t // own_tiles, t % own_tiles : t % own_tiles + 1, :]
-            rmat[t] = w * jnp.exp(top[t] + bias[t] - norm[t : t + 1, :])
+            grow[t] = jnp.broadcast_to(gain[t : t + 1, :], (8, TILE))
         return copies
 
     def spends():
@@ -328,24 +356,27 @@
         for r in range(packed):
 
             def body(t, acc):
-                k0 = kmat[t, r * TILE : r * TILE + width, :]
-                k1 = kmat[t, r * TILE + width : (r + 1) * TILE, :]
-                r0 = rmat[t, 2 * r : 2 * r + 1, :]
-                r1 = rmat[t, 2 * r + 1 : 2 * r + 2, :]
-                return (acc[0] + k0 * r0, acc[1] + k1 * r1)
-
-            zero = jnp.zeros((width, TILE), F32)
+                gain = grow[t]
+                out = []
+                for h in range(2):
+                    first = r * TILE + h * width
+                    k = kmat[t, first : first + width, :].reshape(width // 8, 8, TILE)
+                    out.append(acc[h] + k * (factor[t, 2 * r + h] * gain))
+                return tuple(out)
+
+            zero = jnp.zeros((width // 8, 8, TILE), F32)
             a0, a1 = lax.fori_loop(0, tiles, body, (zero, zero), unroll=4)
-            ones.append(jnp.sum(jnp.transpose(jnp.concatenate([a0, a1], axis=0)), axis=0, keepdims=True))
+            both = jnp.concatenate([a0, a1], axis=0).reshape(TILE, TILE)
+            ones.append(jnp.sum(jnp.transpose(both), axis=0, keepdims=True))
         return ones
 
     for t in range(tiles):
-        lim = top[t] + bias[t]
-        m = jnp.max(lim, axis=0, keepdims=True)
+        lim = top[t]
+        m = jnp.max(jnp.max(lim, axis=0), axis=0, keepdims=True)
         mx_row[t : t + 1, :] = m
         f = jnp.exp(lim - m)
-        rmat[t] = f
-        zt_row[t : t + 1, :] = jnp.sum(f * zsum[t], axis=0, keepdims=True)
+        factor[t] = f
+        zt_row[t : t + 1, :] = jnp.sum(jnp.sum(f * zsum[t], axis=0), axis=0, keepdims=True)
     x_copies = exchange_norms(0)
 
     part1[q] = jnp.concatenate(spends(), axis=0) * v_lane
@@ -361,8 +392,6 @@
         )
         copy.start()
         y_copies.append(copy)
-    for t in range(tiles):
-        rmat[t] = jnp.exp(top[t] + bias[t] - mx_row[t : t + 1, :])
     for k in range(n_chip - 1):
         other = slot_of(*chips[k])
         pltpu.make_async_remote_copy(
@@ -379,15 +408,22 @@
     price = price + STEP_RATE * (jnp.log(goal) - jnp.log(spend + 0.25 * goal))
     v_lane = spread(price)
 
-    def zbody(t, carry):
-        acc = jnp.zeros((8, TILE), F32)
-        for qq in range(n_chip):
-            part = kmat[t, qq * width : (qq + 1) * width, :] * vcol[qq * width : (qq + 1) * width, :]
-            acc = acc + jnp.sum(part.reshape(width // 8, 8, TILE), axis=0) * rmat[t, qq : qq + 1, :]
-        zt_row[pl.ds(t, 1), :] = jnp.sum(acc, axis=0, keepdims=True)
+    group = 4
+
+    def zbody(n, carry):
+        acc = [jnp.zeros((8, TILE), F32)] * group
+        for b in range(n_chip):
+            place = slice(b * width, (b + 1) * width)
+            v = vcol[place, :].reshape(width // 8, 8, TILE)
+            for m in range(group):
+                t = n * group + m
+                part = jnp.sum(kmat[t, place, :].reshape(width // 8, 8, TILE) * v, axis=0)
+                acc[m] = acc[m] + part * factor[t, b]
+        for m in range(group):
+            zt_row[pl.ds(n * group + m, 1), :] = jnp.sum(acc[m], axis=0, keepdims=True)
         return carry
 
-    lax.fori_loop(0, tiles, zbody, 0)
+    lax.fori_loop(0, tiles // group, zbody, 0)
     x_copies += exchange_norms(1)
 
     for r, value in enumerate(spends()):
@@ -417,8 +453,11 @@
             device_id_type=MESH,
         ).wait_recv()
     spend = got2[0]
-    for k in range(1, n_chip):
+    for k in range(1, n_chip // 2):
         spend = spend + got2[k]
+    spend_b = got2[n_chip // 2]
+    for k in range(n_chip // 2 + 1, n_chip):
+        spend_b = spend_b + got2[k]
 
     row = lax.broadcasted_iota(jnp.int32, (packed, TILE), 0)
 
@@ -426,10 +465,9 @@
         return jnp.where(y == 0, value, pltpu.roll(value, width, 1))[:, :width]
 
     price_row = jnp.sum(jnp.where(row == z, price, 0.0), axis=0, keepdims=True)
-    goal_row = jnp.sum(jnp.where(row == z, goal, 0.0), axis=0, keepdims=True)
-    final = price_row + STEP_RATE * (jnp.log(goal_row) - jnp.log(spend + 0.25 * goal_row))
-    spend_ref[...] = own_half(spend)
-    new_price_ref[...] = own_half(final)
+    spend_ref[0:1] = own_half(spend)
+    spend_ref[1:2] = own_half(spend_b)
+    spend_ref[2:3] = own_half(price_row)
 
     for copy in sent + core_copies + pg_copies + x_copies + y_copies:
         copy.wait_send()
@@ -450,11 +488,10 @@
         any_spec = pl.BlockSpec(memory_space=pl.ANY)
         vmem = pl.BlockSpec(memory_space=pltpu.VMEM)
         dma = pltpu.SemaphoreType.DMA
-        new_prices, spend, norms = pl.pallas_call(
+        tail, norms = pl.pallas_call(
             functools.partial(kernel, n_chip, n_cre),
             out_shape=(
-                jax.ShapeDtypeStruct((1, width), F32),
-                jax.ShapeDtypeStruct((1, width), F32),
+                jax.ShapeDtypeStruct((3, width), F32),
                 jax.ShapeDtypeStruct((own_tiles, TILE), F32),
             ),
             in_specs=[
@@ -466,15 +503,16 @@
                 any_spec,
                 any_spec,
             ],
-            out_specs=(vmem, vmem, vmem),
+            out_specs=(vmem, vmem),
             scratch_shapes=[
                 pltpu.VMEM((2 * rows, wide), jnp.bfloat16),
                 pltpu.VMEM((creatives, wide), jnp.bfloat16),
                 pltpu.VMEM((tiles, creatives, TILE), F32),
-                pltpu.VMEM((tiles, n_chip, TILE), F32),
-                pltpu.VMEM((tiles, n_chip, TILE), F32),
-                pltpu.VMEM((tiles, n_chip, TILE), F32),
-                pltpu.VMEM((tiles, n_chip, TILE), F32),
+                pltpu.VMEM((tiles, n_chip, 8, TILE), F32),
+                pltpu.VMEM((tiles, n_chip, 8, TILE), F32),
+                pltpu.VMEM((tiles, n_chip, 8, TILE), F32),
+                pltpu.VMEM((tiles, n_chip, 8, TILE), F32),
+                pltpu.VMEM((tiles, 8, TILE), F32),
                 pltpu.VMEM((creatives, TILE), F32),
                 pltpu.VMEM((2, tiles, TILE), F32),
                 pltpu.VMEM((own_tiles, block_lists.shape[1]), jnp.int32),
@@ -511,7 +549,9 @@
             spend_goals,
             prices,
         )
-        return new_prices, spend, norms.reshape(rows)
+        spend = tail[0:1] + tail[1:2]
+        change = jnp.log(spend_goals) - jnp.log(spend + 0.25 * spend_goals)
+        return tail[2:3] + STEP_RATE * change, spend, norms.reshape(rows)
 
     return jax.shard_map(
         step,

time: 53 us -> 50.6 us (0.955)
  Pallas kernels: 49.9 us -> 47.9 us
  local copies, waits for them, and re-layouts: 2.3 us -> 1.42 us
  other arithmetic: 0 us -> 0.53 us
    pallas_call x1, Pallas kernels: 49.9 us -> 47.9 us  [step(): pl.pallas_call(functools.partial(kernel, n_chip, n_cre), out_shape=(jax.S...]
    unnamed x9 -> x7, local copies, waits for them, and re-layouts: 2.3 us -> 1.42 us
where the time goes in v3:
time: 50.6 us; the launch traced here: 50.5 us
  Pallas kernels  47.9 us (95%)
  local copies, waits for them, and re-layouts  1.42 us (3%)
  between operations  0.66 us (1%)
  other arithmetic  0.53 us (1%)
    pallas_call x1, Pallas kernels, step(): pl.pallas_call(functools.partial(kernel, n_chip, n_cre), out_shape=(jax.S...  47.9 us
    unnamed x7, local copies, waits for them, and re-layouts  1.42 us

profile of v3, /device:TPU:1, one launch (start us, length us, event | category | flops | bytes accessed | tf_op | source)
XLA Modules:
  0.0 50.5 jit_solution(14664411693244488016)
XLA Ops:
  0.6 47.9 %shard_map.94 = (f32[3,64]{1,0:T(4,128)}, f32[8,128]{1,0:T(8,128)}) custom-call(bf16[1024,256]{1,0:T(8,128)(2,1)} %imp_hbm.1, bf16[64,256]{1,0:T(8,128)(2,1)} %bitcast.3, s32[8,16]{1,0:T(8,128)} %list_hbm.1, s32[8]{0:T(128)} %count_ref.1, f32[8,128]{1,0:T(8,128)} %bitcast.4, f32[1,64]{1,0:T(1,128)} %goal_hbm.1, f32[1,64]{1,0:T(1,128)} %price_hbm.1), custom_call_target="tpu_custom_call" | custom-call | tf_op jit(solution)/shard_map/pallas_call | solution.py:491
  48.5 0.0 copy-start.2
  48.5 0.0 copy-start.1
  48.5 0.7 %copy-done.2 = f32[3,64]{1,0:T(4,128)S(1)} copy-done((f32[3,64]{1,0:T(4,128)S(1)}, f32[3,64]{1,0:T(4,128)}, u32[]{:S(2)}) %copy-start.2) | copy-done | bytes 792
  49.2 0.0 copy-done.1
  49.2 0.0 copy-start
  49.2 0.5 %multiply_add_fusion = (f32[1,64]{1,0:T(1,128)}, f32[1,64]{1,0:T(1,128)}) fusion(f32[1,64]{1,0:T(1,128)S(1)} %copy-done.1, f32[3,64]{1,0:T(4,128)S(1)} %copy-done.2), kind=kLoop, calls=%fused_computation | loop fusion | flops 384 | bytes 1536 | tf_op jit(solution)/shard_map/add | solution.py:554
  49.7 0.2 copy-done
  49.9 0.6 %copy.11 = f32[1024]{0:T(1024)} copy(f32[1024]{0:T(1024)S(1)} %bitcast.5) | data formatting | bytes 8192
Async XLA Ops:
  48.5 0.7 %copy-start.2 = (f32[3,64]{1,0:T(4,128)S(1)}, f32[3,64]{1,0:T(4,128)}, u32[]{:S(2)}) copy-start(f32[3,64]{1,0:T(4,128)} %get-tuple-element.5) | copy-start | bytes 2308
  48.5 0.7 %copy-start.1 = (f32[1,64]{1,0:T(1,128)S(1)}, f32[1,64]{1,0:T(1,128)}, u32[]{:S(2)}) copy-start(f32[1,64]{1,0:T(1,128)} %goal_hbm.1) | copy-start | bytes 772
  49.2 0.7 %copy-start = (f32[8,128]{1,0:T(8,128)S(1)}, f32[8,128]{1,0:T(8,128)}, u32[]{:S(2)}) copy-start(f32[8,128]{1,0:T(8,128)} %get-tuple-element.6) | copy-start | bytes 12292

commit v4 on v3

--- a/solution.py
+++ b/solution.py
@@ -49,6 +49,7 @@
     part1,
     part2,
     got2,
+    whole,
     local_sem,
     panel_send,
     panel_recv,
@@ -85,6 +86,9 @@
     def slot_of(step, dy):
         return plane(step) * 2 + (y if dy == 0 else 1 - y)
 
+    def rel(step, dy):
+        return step % nz * 2 + dy
+
     def at(step, dy):
         return {"imp": slot_of(step, dy) * 2 + c, "cre": g if dy == 0 else mirror}
 
@@ -110,14 +114,14 @@
     own_rows = pl.ds(pl.multiple_of(c * rows, rows), rows)
 
     def shard_ref(slot):
-        return panels.at[pl.ds(pl.multiple_of(slot * width, width), width)]
+        return panels.at[pl.ds(slot * width, width)]
 
     local = [
         pltpu.make_async_copy(price_hbm, pg_own.at[0], local_sem.at[0]),
         pltpu.make_async_copy(goal_hbm, pg_own.at[1], local_sem.at[1]),
         pltpu.make_async_copy(list_hbm, lists, local_sem.at[2]),
         pltpu.make_async_copy(weight_hbm, wl.at[c, pl.ds(0, own_tiles)], local_sem.at[3]),
-        pltpu.make_async_copy(panel_hbm, shard_ref(q), local_sem.at[4]),
+        pltpu.make_async_copy(panel_hbm, shard_ref(0), local_sem.at[4]),
         pltpu.make_async_copy(imp_hbm, imps.at[own_rows], local_sem.at[5]),
     ]
     for copy in local:
@@ -125,31 +129,31 @@
 
     for copy in local[:2]:
         copy.wait()
-    pg[q] = jnp.concatenate([pg_own[0], pg_own[1]], axis=1)
+    pg[0] = jnp.concatenate([pg_own[0], pg_own[1]], axis=1)
     pl.semaphore_wait(barrier, len(near) + n_x - 1)
 
     pg_copies = []
 
-    def pg_copy(slot, peer, n=0):
+    def pg_copy(src, dst, peer, n=0):
         return pltpu.make_async_remote_copy(
-            src_ref=pg.at[slot],
-            dst_ref=pg.at[slot],
+            src_ref=pg.at[src],
+            dst_ref=pg.at[dst],
             send_sem=pg_send.at[n],
-            recv_sem=pg_recv.at[slot],
+            recv_sem=pg_recv.at[dst],
             device_id=peer,
             device_id_type=MESH,
         )
 
-    def pg_put(slot, peer):
-        copy = pg_copy(slot, peer, len(pg_copies))
+    def pg_put(src, dst, peer):
+        copy = pg_copy(src, dst, peer, len(pg_copies))
         copy.start()
         pg_copies.append(copy)
 
     def pg_arrived(step, dy):
-        pg_copy(slot_of(step, dy), at(0, 1)).wait_recv()
+        pg_copy(0, rel(step, dy), at(0, 1)).wait_recv()
 
     for step, dy in near:
-        pg_put(q, at(step, dy))
+        pg_put(0, rel(-step, dy), at(step, dy))
 
     sent = []
 
@@ -169,12 +173,12 @@
         sent.append(copy)
 
     def arrived(step, dy):
-        panel_copy(panel_hbm, slot_of(step, dy), at(0, 1)).wait_recv()
+        panel_copy(panel_hbm, rel(step, dy), at(0, 1)).wait_recv()
 
     for step in (2, -2, 1, -1):
         for dy in (1, 0):
-            send(panel_hbm, q, at(step, dy))
-    send(panel_hbm, q, at(0, 1))
+            send(panel_hbm, rel(-step, dy), at(step, dy))
+    send(panel_hbm, rel(0, 1), at(0, 1))
 
     imp_copy = pltpu.make_async_remote_copy(
         src_ref=imp_hbm,
@@ -210,7 +214,9 @@
 
     wl_copy.wait_recv()
     ids = lax.broadcasted_iota(jnp.int32, (n_chip, TILE), 0)
-    ids = ids + jnp.where(lax.rem(ids, 2) == y, g, mirror) * n_chip
+    same = lax.rem(ids, 2) == 0
+    ids = lax.rem(lax.div(ids, 2) + z, nz) * 2
+    ids = ids + jnp.where(same, g * n_chip + y, mirror * n_chip + 1 - y)
     ids = ids.astype(F32)
     for t in range(tiles):
         row = wl[t // own_tiles, own_tiles + t % own_tiles : own_tiles + t % own_tiles + 1, :]
@@ -222,35 +228,44 @@
     for sign in (1, -1):
         for s in range(2):
             dy = s if sign == 1 else 1 - s
-            slot = slot_of(-2 * sign, dy)
+            slot = rel(-2 * sign, dy)
             pg_arrived(-2 * sign, dy)
             if s == 0:
-                pg_put(slot, at(2 * sign, 0))
-            pg_put(slot, at(sign, 0))
+                pg_put(slot, rel(half, dy), at(2 * sign, 0))
+            pg_put(slot, rel(-3 * sign, dy), at(sign, 0))
             arrived(-2 * sign, dy)
             if s == 0:
-                send(shard_ref(slot), slot, at(2 * sign, 0))
-            send(shard_ref(slot), slot, at(sign, 0))
+                send(shard_ref(slot), rel(half, dy), at(2 * sign, 0))
+            send(shard_ref(slot), rel(-3 * sign, dy), at(sign, 0))
 
     low = lax.broadcasted_iota(jnp.int32, (1, TILE), 1) < width
-    def spread(value):
-        v = jnp.exp(value)
-        for r in range(packed):
-            wide = jnp.broadcast_to(v[r : r + 1, :], (TILE, TILE))
-            vcol[r * TILE : (r + 1) * TILE, :] = jnp.transpose(wide)
+    def spread_row(d, row):
+        v = jnp.exp(row)
+        vcol[d * TILE : (d + 1) * TILE, :] = jnp.transpose(jnp.broadcast_to(v, (TILE, TILE)))
         return v
 
-    def spread_slab(zz):
-        row = jnp.where(low, pg[2 * zz], pltpu.roll(pg[2 * zz + 1], width, 1))
-        wide = jnp.broadcast_to(jnp.exp(row), (TILE, TILE))
-        vcol[pl.ds(pl.multiple_of(zz * TILE, TILE), TILE), :] = jnp.transpose(wide)
+    def turned(row):
+        return jnp.where(y == 0, row, pltpu.roll(row, width, 1))
+
+    def plane_row(d):
+        return pl.ds(plane(d), 1)
+
+    values = {}
+
+    def spread_slab(step):
+        d = step % nz
+        even, odd = pg[2 * d], pg[2 * d + 1]
+        row = jnp.where(low, even, pltpu.roll(odd, width, 1))
+        values[d] = spread_row(d, row)
+        whole[0, plane_row(d), :] = turned(row)
+        whole[1, plane_row(d), :] = turned(jnp.where(low, pltpu.roll(even, width, 1), odd))
 
     slab_rows = 2 * width
 
     def process(slabs):
         parts = []
         for zz in slabs:
-            parts.append(panels[pl.ds(pl.multiple_of(zz * slab_rows, slab_rows), slab_rows), :])
+            parts.append(panels[zz * slab_rows : (zz + 1) * slab_rows, :])
         pan = parts[0] if len(parts) == 1 else jnp.concatenate(parts, axis=0)
 
         def body(t2, carry):
@@ -259,7 +274,7 @@
             for n, zz in enumerate(slabs):
                 for h in range(2):
                     qq = zz * 2 + h
-                    place = pl.ds(pl.multiple_of(qq * width, width), width)
+                    place = slice(qq * width, (qq + 1) * width)
                     v = vcol[place, :].reshape(width // 8, 8, TILE)
                     for side in range(2):
                         t = t2 * 2 + side
@@ -279,38 +294,26 @@
         copy.wait()
     imp_copy.wait_recv()
     pg_arrived(0, 1)
-    spread_slab(z)
+    spread_slab(0)
     arrived(0, 1)
-    process([z])
+    process([0])
     for d in range(1, half):
         for step in (d, -d):
             for dy in range(2):
                 if d != 2:
                     pg_arrived(step, dy)
-            spread_slab(plane(step))
+            spread_slab(step)
         for step in (d, -d):
             for dy in range(2):
                 if d != 2:
                     arrived(step, dy)
-        process([plane(d), plane(-d)])
+        process([d, nz - d])
     for dy in range(2):
         pg_arrived(half, dy)
-    spread_slab(plane(half))
+    spread_slab(half)
     for dy in range(2):
         arrived(half, dy)
-    process([plane(half)])
-
-    price_rows = []
-    goal_rows = []
-    for r in range(packed):
-        even = pg[2 * r]
-        odd = pg[2 * r + 1]
-        price_rows.append(jnp.where(low, even, pltpu.roll(odd, width, 1)))
-        goal_rows.append(jnp.where(low, pltpu.roll(even, width, 1), odd))
-    price = jnp.concatenate(price_rows, axis=0)
-    goal = jnp.concatenate(goal_rows, axis=0)
-
-    v_lane = jnp.exp(price)
+    process([half])
 
     def exchange_norms(phase):
         lse[phase, me_x] = mx_row[...] + jnp.log(zt_row[...])
@@ -365,7 +368,7 @@
                 return tuple(out)
 
             zero = jnp.zeros((width // 8, 8, TILE), F32)
-            a0, a1 = lax.fori_loop(0, tiles, body, (zero, zero), unroll=4)
+            a0, a1 = lax.fori_loop(0, tiles, body, (zero, zero), unroll=tiles)
             both = jnp.concatenate([a0, a1], axis=0).reshape(TILE, TILE)
             ones.append(jnp.sum(jnp.transpose(both), axis=0, keepdims=True))
         return ones
@@ -379,7 +382,8 @@
         zt_row[t : t + 1, :] = jnp.sum(jnp.sum(f * zsum[t], axis=0), axis=0, keepdims=True)
     x_copies = exchange_norms(0)
 
-    part1[q] = jnp.concatenate(spends(), axis=0) * v_lane
+    for d, value in enumerate(spends()):
+        part1[q, plane_row(d), :] = turned(value * values[d])
     y_copies = []
     for k in range(n_chip - 1):
         copy = pltpu.make_async_remote_copy(
@@ -405,8 +409,13 @@
     spend = part1[0]
     for k in range(1, n_chip):
         spend = spend + part1[k]
-    price = price + STEP_RATE * (jnp.log(goal) - jnp.log(spend + 0.25 * goal))
-    v_lane = spread(price)
+    goal = whole[1]
+    whole[0] = whole[0] + STEP_RATE * (jnp.log(goal) - jnp.log(spend + 0.25 * goal))
+    for d in range(nz):
+        row = turned(whole[0, plane_row(d), :])
+        values[d] = spread_row(d, row)
+        if d == 0:
+            price_row = row
 
     group = 4
 
@@ -426,48 +435,36 @@
     lax.fori_loop(0, tiles // group, zbody, 0)
     x_copies += exchange_norms(1)
 
-    for r, value in enumerate(spends()):
-        part2[r] = value * v_lane[r : r + 1, :]
-    for k in range(n_chip - 1):
-        other, peer = slot_of(*chips[k]), at(*chips[k])
-        copy = pltpu.make_async_remote_copy(
-            src_ref=part2.at[other // 2],
-            dst_ref=got2.at[q],
-            send_sem=y_send.at[1, k],
-            recv_sem=y_recv.at[1, q],
-            device_id=peer,
+    for d, value in enumerate(spends()):
+        part2[d] = value * values[d]
+
+    def row_copy(step, dy, n):
+        return pltpu.make_async_remote_copy(
+            src_ref=part2.at[step % nz],
+            dst_ref=got2.at[rel(-step, dy)],
+            send_sem=y_send.at[1, n],
+            recv_sem=y_recv.at[1, rel(-step, dy)],
+            device_id=at(step, dy),
             device_id_type=MESH,
         )
+
+    for n, (step, dy) in enumerate(chips):
+        copy = row_copy(step, dy, n)
         copy.start()
         y_copies.append(copy)
-    got2[q] = part2[q // 2]
+    got2[0] = part2[0]
     norm_ref[...] = norms[c]
-    for k in range(n_chip - 1):
-        other = slot_of(*chips[k])
-        pltpu.make_async_remote_copy(
-            src_ref=part2.at[0],
-            dst_ref=got2.at[other],
-            send_sem=y_send.at[1, k],
-            recv_sem=y_recv.at[1, other],
-            device_id=at(*chips[k]),
-            device_id_type=MESH,
-        ).wait_recv()
-    spend = got2[0]
-    for k in range(1, n_chip // 2):
-        spend = spend + got2[k]
-    spend_b = got2[n_chip // 2]
-    for k in range(n_chip // 2 + 1, n_chip):
-        spend_b = spend_b + got2[k]
-
-    row = lax.broadcasted_iota(jnp.int32, (packed, TILE), 0)
-
-    def own_half(value):
-        return jnp.where(y == 0, value, pltpu.roll(value, width, 1))[:, :width]
-
-    price_row = jnp.sum(jnp.where(row == z, price, 0.0), axis=0, keepdims=True)
-    spend_ref[0:1] = own_half(spend)
-    spend_ref[1:2] = own_half(spend_b)
-    spend_ref[2:3] = own_half(price_row)
+    for step, dy in chips:
+        row_copy(-step, dy, 0).wait_recv()
+    sums = []
+    for dy in range(2):
+        total = got2[dy]
+        for d in range(1, nz):
+            total = total + got2[2 * d + dy]
+        sums.append(total)
+    spend_ref[0:1] = sums[0][:, :width]
+    spend_ref[1:2] = pltpu.roll(sums[1], width, 1)[:, :width]
+    spend_ref[2:3] = price_row[:, :width]
 
     for copy in sent + core_copies + pg_copies + x_copies + y_copies:
         copy.wait_send()
@@ -525,6 +522,7 @@
                 pltpu.VMEM((n_chip, n_chip // 2, TILE), F32),
                 pltpu.VMEM((n_chip // 2, 1, TILE), F32),
                 pltpu.VMEM((n_chip, 1, TILE), F32),
+                pltpu.VMEM((2, n_chip // 2, TILE), F32),
                 dma((6,)),
                 dma((n_chip - 1,)),
                 dma((n_chip,)),

time: 50.6 us -> 49.3 us (0.974)
  Pallas kernels: 47.9 us -> 46.6 us
    pallas_call x1, Pallas kernels: 47.9 us -> 46.6 us  [step(): pl.pallas_call(functools.partial(kernel, n_chip, n_cre), out_shape=(jax.S...]
where the time goes in v4:
time: 49.3 us; the launch traced here: 49.2 us
  Pallas kernels  46.6 us (95%)
  local copies, waits for them, and re-layouts  1.42 us (3%)
  between operations  0.66 us (1%)
  other arithmetic  0.53 us (1%)
    pallas_call x1, Pallas kernels, step(): pl.pallas_call(functools.partial(kernel, n_chip, n_cre), out_shape=(jax.S...  46.6 us
    unnamed x7, local copies, waits for them, and re-layouts  1.42 us

profile of v4, /device:TPU:1, one launch (start us, length us, event | category | flops | bytes accessed | tf_op | source)
XLA Modules:
  0.0 49.2 jit_solution(7762847068890325057)
XLA Ops:
  0.6 46.6 %shard_map.94 = (f32[3,64]{1,0:T(4,128)}, f32[8,128]{1,0:T(8,128)}) custom-call(bf16[1024,256]{1,0:T(8,128)(2,1)} %imp_hbm.1, bf16[64,256]{1,0:T(8,128)(2,1)} %bitcast.3, s32[8,16]{1,0:T(8,128)} %list_hbm.1, s32[8]{0:T(128)} %count_ref.1, f32[8,128]{1,0:T(8,128)} %bitcast.4, f32[1,64]{1,0:T(1,128)} %goal_hbm.1, f32[1,64]{1,0:T(1,128)} %price_hbm.1), custom_call_target="tpu_custom_call" | custom-call | tf_op jit(solution)/shard_map/pallas_call | solution.py:488
  47.2 0.0 copy-start.2
  47.2 0.0 copy-start.1
  47.2 0.7 %copy-done.2 = f32[3,64]{1,0:T(4,128)S(1)} copy-done((f32[3,64]{1,0:T(4,128)S(1)}, f32[3,64]{1,0:T(4,128)}, u32[]{:S(2)}) %copy-start.2) | copy-done | bytes 792
  47.9 0.0 copy-done.1
  47.9 0.0 copy-start
  47.9 0.5 %multiply_add_fusion = (f32[1,64]{1,0:T(1,128)}, f32[1,64]{1,0:T(1,128)}) fusion(f32[1,64]{1,0:T(1,128)S(1)} %copy-done.1, f32[3,64]{1,0:T(4,128)S(1)} %copy-done.2), kind=kLoop, calls=%fused_computation | loop fusion | flops 384 | bytes 1536 | tf_op jit(solution)/shard_map/add | solution.py:552
  48.4 0.2 copy-done
  48.6 0.6 %copy.11 = f32[1024]{0:T(1024)} copy(f32[1024]{0:T(1024)S(1)} %bitcast.5) | data formatting | bytes 8192
Async XLA Ops:
  47.2 0.7 %copy-start.2 = (f32[3,64]{1,0:T(4,128)S(1)}, f32[3,64]{1,0:T(4,128)}, u32[]{:S(2)}) copy-start(f32[3,64]{1,0:T(4,128)} %get-tuple-element.5) | copy-start | bytes 2308
  47.2 0.7 %copy-start.1 = (f32[1,64]{1,0:T(1,128)S(1)}, f32[1,64]{1,0:T(1,128)}, u32[]{:S(2)}) copy-start(f32[1,64]{1,0:T(1,128)} %goal_hbm.1) | copy-start | bytes 772
  47.9 0.7 %copy-start = (f32[8,128]{1,0:T(8,128)S(1)}, f32[8,128]{1,0:T(8,128)}, u32[]{:S(2)}) copy-start(f32[8,128]{1,0:T(8,128)} %get-tuple-element.6) | copy-start | bytes 12292

commit v5 on v4

--- a/solution.py
+++ b/solution.py
@@ -27,6 +27,7 @@
     weight_hbm,
     goal_hbm,
     price_hbm,
+    new_price_ref,
     spend_ref,
     norm_ref,
     imps,
@@ -315,7 +316,12 @@
         arrived(half, dy)
     process([half])
 
-    def exchange_norms(phase):
+    def drain(*groups):
+        for group in groups:
+            for copy in group:
+                copy.wait_send()
+
+    def exchange_norms(phase, earlier):
         lse[phase, me_x] = mx_row[...] + jnp.log(zt_row[...])
         copies = []
         for k in far_first:
@@ -329,6 +335,7 @@
             )
             copy.start()
             copies.append(copy)
+        drain(*earlier)
         for k in range(1, n_x):
             other = lax.rem(me_x + k, n_x)
             pltpu.make_async_remote_copy(
@@ -380,7 +387,7 @@
         f = jnp.exp(lim - m)
         factor[t] = f
         zt_row[t : t + 1, :] = jnp.sum(jnp.sum(f * zsum[t], axis=0), axis=0, keepdims=True)
-    x_copies = exchange_norms(0)
+    x_copies = exchange_norms(0, (sent, core_copies, pg_copies))
 
     for d, value in enumerate(spends()):
         part1[q, plane_row(d), :] = turned(value * values[d])
@@ -396,6 +403,7 @@
         )
         copy.start()
         y_copies.append(copy)
+    drain(x_copies)
     for k in range(n_chip - 1):
         other = slot_of(*chips[k])
         pltpu.make_async_remote_copy(
@@ -433,7 +441,7 @@
         return carry
 
     lax.fori_loop(0, tiles // group, zbody, 0)
-    x_copies += exchange_norms(1)
+    x_last = exchange_norms(1, (y_copies,))
 
     for d, value in enumerate(spends()):
         part2[d] = value * values[d]
@@ -448,10 +456,12 @@
             device_id_type=MESH,
         )
 
+    y_last = []
     for n, (step, dy) in enumerate(chips):
         copy = row_copy(step, dy, n)
         copy.start()
-        y_copies.append(copy)
+        y_last.append(copy)
+    drain(x_last)
     got2[0] = part2[0]
     norm_ref[...] = norms[c]
     for step, dy in chips:
@@ -462,12 +472,22 @@
         for d in range(1, nz):
             total = total + got2[2 * d + dy]
         sums.append(total)
-    spend_ref[0:1] = sums[0][:, :width]
-    spend_ref[1:2] = pltpu.roll(sums[1], width, 1)[:, :width]
-    spend_ref[2:3] = price_row[:, :width]
-
-    for copy in sent + core_copies + pg_copies + x_copies + y_copies:
-        copy.wait_send()
+    spend = (sums[0] + pltpu.roll(sums[1], width, 1))[:, :width]
+    goal = pg_own[1]
+    change = jnp.log(goal) - jnp.log(spend + 0.25 * goal)
+    spend_ref[...] = spend
+    new_price_ref[...] = price_row[:, :width] + STEP_RATE * change
+
+    drain(y_last)
+
+
+def hand_on(price_ref, spend_ref, norm_ref, price_out, spend_out, norm_out, sem):
+    pairs = ((price_ref, price_out), (spend_ref, spend_out), (norm_ref, norm_out))
+    copies = [pltpu.make_async_copy(a, b, sem.at[n]) for n, (a, b) in enumerate(pairs)]
+    for copy in copies:
+        copy.start()
+    for copy in copies:
+        copy.wait()
 
 
 def solution(mesh):
@@ -485,10 +505,11 @@
         any_spec = pl.BlockSpec(memory_space=pl.ANY)
         vmem = pl.BlockSpec(memory_space=pltpu.VMEM)
         dma = pltpu.SemaphoreType.DMA
-        tail, norms = pl.pallas_call(
+        results = pl.pallas_call(
             functools.partial(kernel, n_chip, n_cre),
             out_shape=(
-                jax.ShapeDtypeStruct((3, width), F32),
+                jax.ShapeDtypeStruct((1, width), F32),
+                jax.ShapeDtypeStruct((1, width), F32),
                 jax.ShapeDtypeStruct((own_tiles, TILE), F32),
             ),
             in_specs=[
@@ -500,7 +521,7 @@
                 any_spec,
                 any_spec,
             ],
-            out_specs=(vmem, vmem),
+            out_specs=(vmem, vmem, vmem),
             scratch_shapes=[
                 pltpu.VMEM((2 * rows, wide), jnp.bfloat16),
                 pltpu.VMEM((creatives, wide), jnp.bfloat16),
@@ -547,9 +568,15 @@
             spend_goals,
             prices,
         )
-        spend = tail[0:1] + tail[1:2]
-        change = jnp.log(spend_goals) - jnp.log(spend + 0.25 * spend_goals)
-        return tail[2:3] + STEP_RATE * change, spend, norms.reshape(rows)
+        new_prices, spend, norms = pl.pallas_call(
+            hand_on,
+            out_shape=tuple(jax.ShapeDtypeStruct(x.shape, x.dtype) for x in results),
+            in_specs=[any_spec] * 3,
+            out_specs=(any_spec,) * 3,
+            scratch_shapes=[dma((3,))],
+            compiler_params=pltpu.CompilerParams(vmem_limit_bytes=63 << 20),
+        )(*results)
+        return new_prices, spend, norms.reshape(rows)
 
     return jax.shard_map(
         step,

time: 49.3 us -> 48.5 us (0.984)
  local copies, waits for them, and re-layouts: 1.42 us -> 0 us
  Pallas kernels: 46.6 us -> 47.7 us
  other arithmetic: 0.53 us -> 0 us
    unnamed x7 -> x0, local copies, waits for them, and re-layouts: 1.42 us -> none
    pallas_call x0 -> x1, Pallas kernels: none -> 1.29 us  [step(): pl.pallas_call(hand_on, out_shape=tuple((jax.ShapeDtypeStruct(x.shape, x....]
    add x1 -> x0, other arithmetic: 0.53 us -> none  [step(): return (tail[2:3] + STEP_RATE * change, spend, norms.reshape(rows))]
where the time goes in v5:
time: 48.5 us; the launch traced here: 48.4 us
  Pallas kernels  47.7 us (98%)
  between operations  0.64 us (1%)
    pallas_call x1, Pallas kernels, step(): pl.pallas_call(functools.partial(kernel, n_chip, n_cre), out_shape=(jax.S...  46.5 us
    pallas_call x1, Pallas kernels, step(): pl.pallas_call(hand_on, out_shape=tuple((jax.ShapeDtypeStruct(x.shape, x....  1.29 us

profile of v5, /device:TPU:1, one launch (start us, length us, event | category | flops | bytes accessed | tf_op | source)
XLA Modules:
  0.0 48.4 jit_solution(17140575811389280265)
XLA Ops:
  0.6 46.5 %shard_map.94 = (f32[1,64]{1,0:T(1,128)}, f32[1,64]{1,0:T(1,128)}, f32[8,128]{1,0:T(8,128)}) custom-call(bf16[1024,256]{1,0:T(8,128)(2,1)} %imp_hbm.1, bf16[64,256]{1,0:T(8,128)(2,1)} %bitcast.3, s32[8,16]{1,0:T(8,128)} %list_hbm.1, s32[8]{0:T(128)} %count_ref.1, f32[8,128]{1,0:T(8,128)} %bitcast.4, f32[1,64]{1,0:T(1,128)} %goal_hbm.1, f32[1,64]{1,0:T(1,128)} %price_hbm.1), custom_call_target="tpu_custom_call" | custom-call | tf_op jit(solution)/shard_map/pallas_call | solution.py:508
  47.1 1.3 %shard_map.95 = (f32[1,64]{1,0:T(1,128)}, f32[1,64]{1,0:T(1,128)}, f32[8,128]{1,0:T(8,128)}) custom-call(f32[1,64]{1,0:T(1,128)} %get-tuple-element.9.price_ref, f32[1,64]{1,0:T(1,128)} %get-tuple-element.10.spend_ref, f32[8,128]{1,0:T(8,128)} %get-tuple-element.11.norm_ref), custom_call_target="tpu_custom_call" | custom-call | tf_op jit(solution)/shard_map/pallas_call | solution.py:571

commit v6 on v5

--- a/solution.py
+++ b/solution.py
@@ -98,11 +98,23 @@
         chips += [(d, 1), (-d, 1), (d, 0), (-d, 0)]
     chips += [(0, 1)]
 
+    x_half = n_cre // 4
+    cres = [(x_half, dl, dc) for dl in (1, 0) for dc in (1, 0)]
+    for d in range(x_half - 1, 0, -1):
+        cres += [(s, dl, dc) for dl in (1, 0) for s in (d, -d) for dc in (1, 0)]
+    cres += [(0, 1, 1), (0, 1, 0), (0, 0, 1)]
+
+    def cre_slot(k):
+        dx, dl, dc = cres[k - 1]
+        line = lax.rem(g // 2 + dx + n_cre // 2, n_cre // 2)
+        side = lax.rem(g + dl, 2)
+        return line * 4 + side * 2 + lax.rem(c + dc, 2)
+
     def cre_peer(k):
-        other = lax.rem(me_x + k, n_x)
+        other = cre_slot(k)
         return {"imp": q * 2 + lax.rem(other, 2), "cre": other // 2}
 
-    far_first = sorted(range(1, n_x), key=lambda k: -min(k, n_x - k))
+    far_first = range(1, n_x)
     core_peer = {"imp": q * 2 + 1 - c, "cre": g}
 
     barrier = pltpu.get_barrier_semaphore()
@@ -308,13 +320,14 @@
             for dy in range(2):
                 if d != 2:
                     arrived(step, dy)
-        process([d, nz - d])
+        if d + 1 < half:
+            process([d, nz - d])
     for dy in range(2):
         pg_arrived(half, dy)
     spread_slab(half)
     for dy in range(2):
         arrived(half, dy)
-    process([half])
+    process([half - 1, half + 1, half])
 
     def drain(*groups):
         for group in groups:
@@ -337,7 +350,7 @@
             copies.append(copy)
         drain(*earlier)
         for k in range(1, n_x):
-            other = lax.rem(me_x + k, n_x)
+            other = cre_slot(k)
             pltpu.make_async_remote_copy(
                 src_ref=lse.at[phase, me_x],
                 dst_ref=lse.at[phase, other],

time: 48.5 us -> 47.9 us (0.988)
  Pallas kernels: 47.7 us -> 47.1 us
    pallas_call x1, Pallas kernels: 46.5 us -> 45.8 us  [step(): pl.pallas_call(functools.partial(kernel, n_chip, n_cre), out_shape=(jax.S...]
where the time goes in v6:
time: 47.9 us; the launch traced here: 47.8 us
  Pallas kernels  47.1 us (98%)
  between operations  0.64 us (1%)
    pallas_call x1, Pallas kernels, step(): pl.pallas_call(functools.partial(kernel, n_chip, n_cre), out_shape=(jax.S...  45.8 us
    pallas_call x1, Pallas kernels, step(): pl.pallas_call(hand_on, out_shape=tuple((jax.ShapeDtypeStruct(x.shape, x....  1.29 us

profile of v6, /device:TPU:1, one launch (start us, length us, event | category | flops | bytes accessed | tf_op | source)
XLA Modules:
  0.0 47.8 jit_solution(3575496462556126983)
XLA Ops:
  0.6 45.8 %shard_map.94 = (f32[1,64]{1,0:T(1,128)}, f32[1,64]{1,0:T(1,128)}, f32[8,128]{1,0:T(8,128)}) custom-call(bf16[1024,256]{1,0:T(8,128)(2,1)} %imp_hbm.1, bf16[64,256]{1,0:T(8,128)(2,1)} %bitcast.3, s32[8,16]{1,0:T(8,128)} %list_hbm.1, s32[8]{0:T(128)} %count_ref.1, f32[8,128]{1,0:T(8,128)} %bitcast.4, f32[1,64]{1,0:T(1,128)} %goal_hbm.1, f32[1,64]{1,0:T(1,128)} %price_hbm.1), custom_call_target="tpu_custom_call" | custom-call | tf_op jit(solution)/shard_map/pallas_call | solution.py:521
  46.5 1.3 %shard_map.95 = (f32[1,64]{1,0:T(1,128)}, f32[1,64]{1,0:T(1,128)}, f32[8,128]{1,0:T(8,128)}) custom-call(f32[1,64]{1,0:T(1,128)} %get-tuple-element.9.price_ref, f32[1,64]{1,0:T(1,128)} %get-tuple-element.10.spend_ref, f32[8,128]{1,0:T(8,128)} %get-tuple-element.11.norm_ref), custom_call_target="tpu_custom_call" | custom-call | tf_op jit(solution)/shard_map/pallas_call | solution.py:584

commit v7 on v6

--- a/solution.py
+++ b/solution.py
@@ -117,13 +117,6 @@
     far_first = range(1, n_x)
     core_peer = {"imp": q * 2 + 1 - c, "cre": g}
 
-    barrier = pltpu.get_barrier_semaphore()
-    near = [(step, dy) for step, dy in chips if abs(step) <= 2]
-    for step, dy in near:
-        pl.semaphore_signal(barrier, inc=1, device_id=at(step, dy), device_id_type=MESH)
-    for k in far_first:
-        pl.semaphore_signal(barrier, inc=1, device_id=cre_peer(k), device_id_type=MESH)
-
     own_rows = pl.ds(pl.multiple_of(c * rows, rows), rows)
 
     def shard_ref(slot):
@@ -137,7 +130,17 @@
         pltpu.make_async_copy(panel_hbm, shard_ref(0), local_sem.at[4]),
         pltpu.make_async_copy(imp_hbm, imps.at[own_rows], local_sem.at[5]),
     ]
-    for copy in local:
+    for copy in local[:2]:
+        copy.start()
+
+    barrier = pltpu.get_barrier_semaphore()
+    near = [(step, dy) for step, dy in chips if abs(step) <= 2]
+    for step, dy in near:
+        pl.semaphore_signal(barrier, inc=1, device_id=at(step, dy), device_id_type=MESH)
+    for k in far_first:
+        pl.semaphore_signal(barrier, inc=1, device_id=cre_peer(k), device_id_type=MESH)
+
+    for copy in local[2:]:
         copy.start()
 
     for copy in local[:2]:

time: 47.9 us -> 47.9 us (level)
  no operation moved by 1% of the time
where the time goes in v7:
time: 47.9 us; the launch traced here: 47.8 us
  Pallas kernels  47.1 us (98%)
  between operations  0.64 us (1%)
    pallas_call x1, Pallas kernels, step(): pl.pallas_call(functools.partial(kernel, n_chip, n_cre), out_shape=(jax.S...  45.8 us
    pallas_call x1, Pallas kernels, step(): pl.pallas_call(hand_on, out_shape=tuple((jax.ShapeDtypeStruct(x.shape, x....  1.29 us

profile of v7, /device:TPU:1, one launch (start us, length us, event | category | flops | bytes accessed | tf_op | source)
XLA Modules:
  0.0 47.8 jit_solution(16593810054466899917)
XLA Ops:
  0.6 45.8 %shard_map.94 = (f32[1,64]{1,0:T(1,128)}, f32[1,64]{1,0:T(1,128)}, f32[8,128]{1,0:T(8,128)}) custom-call(bf16[1024,256]{1,0:T(8,128)(2,1)} %imp_hbm.1, bf16[64,256]{1,0:T(8,128)(2,1)} %bitcast.3, s32[8,16]{1,0:T(8,128)} %list_hbm.1, s32[8]{0:T(128)} %count_ref.1, f32[8,128]{1,0:T(8,128)} %bitcast.4, f32[1,64]{1,0:T(1,128)} %goal_hbm.1, f32[1,64]{1,0:T(1,128)} %price_hbm.1), custom_call_target="tpu_custom_call" | custom-call | tf_op jit(solution)/shard_map/pallas_call | solution.py:524
  46.5 1.3 %shard_map.95 = (f32[1,64]{1,0:T(1,128)}, f32[1,64]{1,0:T(1,128)}, f32[8,128]{1,0:T(8,128)}) custom-call(f32[1,64]{1,0:T(1,128)} %get-tuple-element.9.price_ref, f32[1,64]{1,0:T(1,128)} %get-tuple-element.10.spend_ref, f32[8,128]{1,0:T(8,128)} %get-tuple-element.11.norm_ref), custom_call_target="tpu_custom_call" | custom-call | tf_op jit(solution)/shard_map/pallas_call | solution.py:587
